TPU v7x, 128 devices: a whole 4x4x4 slice. The times are simulated.
128 devices in a mesh: gx: 16 (over z, x_hi, core), gy: 8 (over x_lo, y).
Axes of the slice: x: 4 (x_hi: 2, x_lo: 2; x = x_hi * 2 + x_lo), y: 4, z: 4, core: 2. Of those that a mesh axis runs over, the one named last changes fastest.
Arguments:
- right_side: float32 [2, 2, 256, 128, 128], P(None, None, 'gx', 'gy'), may hold values from -7 to 7
- slowness: float32 [256, 128, 128], P('gx', 'gy'), may hold values from 0.7 to 1.4
- source_cells: int32 [2, 16], replicated, may hold values from 0 to 4194303
- source_amplitudes: float32 [2, 16, 2], replicated, may hold values from -24 to 24
Outputs:
- wavefield: float32 [2, 2, 256, 128, 128], P(None, None, 'gx', 'gy')
- residual: float32 [2, 2, 256, 128, 128], P(None, None, 'gx', 'gy')
Inputs may be any that keep to these rules, and one draw needn't show every extreme that they name: `source_cells`: flat indices (x * 128 + y) * 128 + z of cells; points may coincide.
All inputs are finite; a program needn't handle non-finite values.
Results may differ from a plain program's by a relative error of at most 0.0003.
Values sent between devices are 32-bit elements; how exact they have to be, the bound alone decides.
A program may use at most 64 MiB of HBM per device.

v0:
```python
import math

import jax
import jax.numpy as jnp
from jax import lax
from jax.sharding import PartitionSpec as P

KAPPA = 0.12
DAMPING = 0.3
HIGHEST = lax.Precision.HIGHEST


def passed_along(array, axis, by):
    size = lax.axis_size(axis)
    pairs = [(i, i + by) for i in range(size) if 0 <= i + by < size]
    return lax.ppermute(array, axis, pairs)


def sine_basis(length):
    positions = jnp.arange(1, length + 1).astype(jnp.float32)
    angles = positions * (math.pi / (length + 1))
    sine_rows = math.sqrt(2.0 / (length + 1)) * jnp.sin(angles[:, None] * positions[None, :])
    return (sine_rows, angles)


def build_tables(size_x, size_y, cells_z):
    sine_x, angle_x = sine_basis(size_x)
    sine_y, angle_y = sine_basis(size_y)
    sine_z, angle_z = sine_basis(cells_z)
    symbol_x = 2.5 - 8.0 / 3.0 * jnp.cos(angle_x) + 1.0 / 6.0 * jnp.cos(2.0 * angle_x)
    symbol_y = 2.5 - 8.0 / 3.0 * jnp.cos(angle_y) + 1.0 / 6.0 * jnp.cos(2.0 * angle_y)
    symbol_z = 2.0 - 2.0 * jnp.cos(angle_z)
    real_part = symbol_x[:, None, None] + symbol_y[None, :, None] + symbol_z[None, None, :] - KAPPA
    denominator = real_part * real_part + (KAPPA * DAMPING) ** 2
    return (sine_x, sine_y, sine_z, real_part / denominator, KAPPA * DAMPING / denominator)


def transform(wavefield, sine_x, sine_y, sine_z):
    result = jnp.einsum("scxyz,zw->scxyw", wavefield, sine_z, precision=HIGHEST)
    result = jnp.einsum("scxyz,xa->scayz", result, sine_x, precision=HIGHEST)
    return jnp.einsum("scxyz,yb->scxbz", result, sine_y, precision=HIGHEST)


def fast_solve(wavefield, tables):
    sine_x, sine_y, sine_z, inverse_real, inverse_imag = tables
    spectrum = transform(wavefield, sine_x, sine_y, sine_z)
    real_part = inverse_real * spectrum[:, 0] - inverse_imag * spectrum[:, 1]
    imag_part = inverse_real * spectrum[:, 1] + inverse_imag * spectrum[:, 0]
    return transform(jnp.stack([real_part, imag_part], axis=1), sine_x, sine_y, sine_z)


def apply_operator(padded, slowness):
    size_x = padded.shape[2] - 4
    size_y = padded.shape[3] - 4
    center = padded[:, :, 2 : 2 + size_x, 2 : 2 + size_y]
    weights = (1.0, -16.0, 30.0, -16.0, 1.0)
    lateral = jnp.zeros_like(center)
    for offset in range(5):
        lateral = lateral + weights[offset] / 12.0 * (
            padded[:, :, offset : offset + size_x, 2 : 2 + size_y]
            + padded[:, :, 2 : 2 + size_x, offset : offset + size_y]
        )
    vertical = jnp.pad(center, ((0, 0), (0, 0), (0, 0), (0, 0), (1, 1)))
    lateral = lateral + 2.0 * center - vertical[..., :-2] - vertical[..., 2:]
    scaled = KAPPA * slowness
    real_part = lateral[:, 0] - scaled * (center[:, 0] - DAMPING * center[:, 1])
    imag_part = lateral[:, 1] - scaled * (center[:, 1] + DAMPING * center[:, 0])
    return jnp.stack([real_part, imag_part], axis=1)


def tile_solve(source_term, trace_x, trace_y, slowness, tables):
    source_term = source_term.at[:, :, 0].add((16.0 * trace_x[:, :, 1] - trace_x[:, :, 0]) / 12.0)
    source_term = source_term.at[:, :, 1].add(-trace_x[:, :, 1] / 12.0)
    source_term = source_term.at[:, :, :, 0].add(
        (16.0 * trace_y[:, :, :, 1] - trace_y[:, :, :, 0]) / 12.0
    )
    source_term = source_term.at[:, :, :, 1].add(-trace_y[:, :, :, 1] / 12.0)
    wavefield = fast_solve(source_term, tables)
    for sweep_step in range(2):
        padded = jnp.pad(wavefield, ((0, 0), (0, 0), (2, 2), (2, 2), (0, 0)))
        wavefield = wavefield + fast_solve(source_term - apply_operator(padded, slowness), tables)
    return wavefield


def point_sources(flat_cells, amplitudes, start_x, start_y, size_x, size_y, cells_z, total_y):
    plane_cells = total_y * cells_z
    coord_x = flat_cells // plane_cells - start_x
    coord_y = flat_cells // cells_z % total_y - start_y
    coord_z = flat_cells % cells_z
    match_x = (coord_x[:, :, None] == jnp.arange(size_x, dtype=jnp.int32)[None, None, :]).astype(
        jnp.float32
    )
    match_y = (coord_y[:, :, None] == jnp.arange(size_y, dtype=jnp.int32)[None, None, :]).astype(
        jnp.float32
    )
    match_z = (coord_z[:, :, None] == jnp.arange(cells_z, dtype=jnp.int32)[None, None, :]).astype(
        jnp.float32
    )
    return jnp.einsum(
        "spc,spx,spy,spz->scxyz", amplitudes, match_x, match_y, match_z, precision=HIGHEST
    )


def body(right_side, slowness, source_cells, source_amplitudes):
    sources = right_side.shape[0]
    size_x = right_side.shape[2]
    size_y = right_side.shape[3]
    cells_z = right_side.shape[4]
    grid_rows = lax.axis_size("gx")
    grid_cols = lax.axis_size("gy")
    tile_row = lax.axis_index("gx")
    tile_col = lax.axis_index("gy")
    forcing = right_side + point_sources(
        source_cells,
        source_amplitudes,
        tile_row * size_x,
        tile_col * size_y,
        size_x,
        size_y,
        cells_z,
        size_y * grid_cols,
    )
    tables = build_tables(size_x, size_y, cells_z)
    wavefield = jnp.zeros_like(forcing)
    trace_x = jnp.zeros((sources, 2, 2, size_y, cells_z), jnp.float32)
    trace_y = jnp.zeros((sources, 2, size_x, 2, cells_z), jnp.float32)

    def advance(beat_index, loop_state):
        current, prior_x, prior_y, outbound_x, outbound_y = loop_state
        inbound_x = passed_along(outbound_x, "gx", 1)
        inbound_y = passed_along(outbound_y, "gy", 1)
        slot_index = beat_index - tile_row - tile_col
        active = jnp.logical_and(slot_index >= 0, slot_index < sources)
        clamped = jnp.clip(slot_index, 0, sources - 1)
        solved = tile_solve(
            lax.dynamic_slice_in_dim(forcing, clamped, 1, 0), inbound_x, inbound_y, slowness, tables
        )
        solved = jnp.where(active, solved, lax.dynamic_slice_in_dim(current, clamped, 1, 0))
        kept_x = jnp.where(active, inbound_x, lax.dynamic_slice_in_dim(prior_x, clamped, 1, 0))
        kept_y = jnp.where(active, inbound_y, lax.dynamic_slice_in_dim(prior_y, clamped, 1, 0))
        current = lax.dynamic_update_slice_in_dim(current, solved, clamped, 0)
        prior_x = lax.dynamic_update_slice_in_dim(prior_x, kept_x, clamped, 0)
        prior_y = lax.dynamic_update_slice_in_dim(prior_y, kept_y, clamped, 0)
        return (
            current,
            prior_x,
            prior_y,
            solved[:, :, size_x - 2 :],
            solved[:, :, :, size_y - 2 :],
        )

    start_x = jnp.zeros((1, 2, 2, size_y, cells_z), jnp.float32)
    start_y = jnp.zeros((1, 2, size_x, 2, cells_z), jnp.float32)
    wavefield, trace_x, trace_y, start_x, start_y = lax.fori_loop(
        0,
        grid_rows + grid_cols + sources - 2,
        advance,
        (wavefield, trace_x, trace_y, start_x, start_y),
    )
    after_x = passed_along(wavefield[:, :, :2], "gx", -1)
    after_y = passed_along(wavefield[:, :, :, :2], "gy", -1)
    padded = jnp.concatenate([trace_x, wavefield, after_x], axis=2)
    before_side = jnp.pad(trace_y, ((0, 0), (0, 0), (2, 2), (0, 0), (0, 0)))
    after_side = jnp.pad(after_y, ((0, 0), (0, 0), (2, 2), (0, 0), (0, 0)))
    padded = jnp.concatenate([before_side, padded, after_side], axis=3)
    residual = forcing - apply_operator(padded, slowness)
    return (wavefield, residual)


def solution(mesh):
    return jax.shard_map(
        body,
        mesh=mesh,
        in_specs=(P(None, None, "gx", "gy", None), P("gx", "gy", None), P(), P()),
        out_specs=(P(None, None, "gx", "gy", None), P(None, None, "gx", "gy", None)),
        check_vma=False,
    )
```

profile of v0, /device:TPU:6, one launch (start us, length us, event | category | flops | bytes accessed | tf_op | source)
XLA Modules:
  0.0 541.2 jit_solution(293489140165976904)
XLA Ops:
  5.4 522.4 %while.31 = (s32[]{:T(128)}, f32[2,2,16,16,128]{4,3,2,1,0:T(8,128)S(1)}, f32[2,2,2,16,128]{4,2,1,3,0:T(2,128)S(1)}, f32[2,2,16,2,128]{4,2,1,3,0:T(8,128)S(1)}, f...) while((s32[]{:T(128)}, ...), condition=%wide.region_1.2_spmd.clone.clone.clone, body=%wide.region_0.1_spmd.clone.clone.clone.sunk | while | flops 760035328 | bytes 20033912 | solution.py:154
  7.3 3.5 collective-permute-start.1
  12.1 3.1 collective-permute-done.1
  26.6 3.6 collective-permute-start
  33.4 4.9 collective-permute-done.1
  53.8 2.7 collective-permute-done
  56.5 3.2 collective-permute-done.1
  71.2 3.0 collective-permute-start
  77.9 4.2 collective-permute-done.1
  97.6 2.7 collective-permute-done
  100.3 3.2 collective-permute-done.1
  115.0 3.4 collective-permute-start
  121.7 4.6 collective-permute-done.1
  141.9 2.7 collective-permute-done
  144.6 3.2 collective-permute-done.1
  159.2 3.0 collective-permute-start
  166.0 4.2 collective-permute-done.1
  185.7 2.7 collective-permute-done
  188.4 3.2 collective-permute-done.1
  203.0 3.1 collective-permute-start
  209.8 4.4 collective-permute-done.1
  229.6 2.7 collective-permute-done
  232.3 3.2 collective-permute-done.1
  247.0 2.7 collective-permute-start
  253.7 3.9 collective-permute-done.1
  275.8 3.5 collective-permute-done.1
  290.8 2.4 collective-permute-start
  297.6 3.6 collective-permute-done.1
  312.6 2.4 collective-permute-start
  319.4 3.6 collective-permute-done.1
  338.7 2.5 collective-permute-done
  341.2 3.4 collective-permute-done.1
  362.8 3.5 collective-permute-done.1
  384.5 3.6 collective-permute-done.1
  403.6 2.7 collective-permute-done
  406.3 3.5 collective-permute-done.1
  425.3 2.7 collective-permute-done
  428.0 3.2 collective-permute-done.1
  446.6 2.8 collective-permute-done
  449.4 3.1 collective-permute-done.1
  467.9 2.8 collective-permute-done
  470.7 3.1 collective-permute-done.1
  489.2 2.8 collective-permute-done
  492.0 3.1 collective-permute-done.1
  510.5 2.8 collective-permute-done
  513.3 3.1 collective-permute-done.1
  528.6 4.4 collective-permute-start.2
  535.0 4.1 collective-permute-done.3
  (1192 shorter events, 377.6 us)
Async XLA Ops:
  5.4 6.7 %collective-permute-start = (f32[1,2,2,16,128]{4,3,2,1,0:T(8,128)S(1)}, f32[1,2,2,16,128]{4,3,2,1,0:T(8,128)S(1)}, u32[]{:S(2)}, u32[]{:S(2)}) collective-permute-start(f32[1,2,2,16,128]{4,3,2,1,0:T(8,128)S(1)} %get-tuple-element.950), channel_id=1, source_target_pairs={{0,8},{8,16},{16,24},{24,32},{32,40},{40,48},{48,56},{56,64},{64,7... | collective-permute-start | bytes 98312 | tf_op jit(solution)/shard_map/while/body/eval_jaxpr/ppermute | solution.py:16
  7.3 7.9 %collective-permute-start.1 = (f32[1,2,16,2,128]{4,3,2,1,0:T(2,128)S(1)}, f32[1,2,16,2,128]{4,3,2,1,0:T(2,128)S(1)}, u32[]{:S(2)}, u32[]{:S(2)}) collective-permute-start(f32[1,2,16,2,128]{4,3,2,1,0:T(2,128)S(1)} %get-tuple-element.951), channel_id=1, source_target_pairs={{0,1},{1,2},{2,3},{3,4},{4,5},{5,6},{6,7},{8,9},{9,10},{10,11},{11... | collective-permute-start | bytes 98312 | tf_op jit(solution)/shard_map/while/body/eval_jaxpr/ppermute | solution.py:16
  26.6 6.7 %collective-permute-start = (f32[1,2,2,16,128]{4,3,2,1,0:T(8,128)S(1)}, f32[1,2,2,16,128]{4,3,2,1,0:T(8,128)S(1)}, u32[]{:S(2)}, u32[]{:S(2)}) collective-permute-start(f32[1,2,2,16,128]{4,3,2,1,0:T(8,128)S(1)} %get-tuple-element.950), channel_id=1, source_target_pairs={{0,8},{8,16},{16,24},{24,32},{32,40},{40,48},{48,56},{56,64},{64,7... | collective-permute-start | bytes 98312 | tf_op jit(solution)/shard_map/while/body/eval_jaxpr/ppermute | solution.py:16
  30.3 8.1 %collective-permute-start.1 = (f32[1,2,16,2,128]{4,3,2,1,0:T(2,128)S(1)}, f32[1,2,16,2,128]{4,3,2,1,0:T(2,128)S(1)}, u32[]{:S(2)}, u32[]{:S(2)}) collective-permute-start(f32[1,2,16,2,128]{4,3,2,1,0:T(2,128)S(1)} %get-tuple-element.951), channel_id=1, source_target_pairs={{0,1},{1,2},{2,3},{3,4},{4,5},{5,6},{6,7},{8,9},{9,10},{10,11},{11... | collective-permute-start | bytes 98312 | tf_op jit(solution)/shard_map/while/body/eval_jaxpr/ppermute | solution.py:16
  49.8 6.7 %collective-permute-start = (f32[1,2,2,16,128]{4,3,2,1,0:T(8,128)S(1)}, f32[1,2,2,16,128]{4,3,2,1,0:T(8,128)S(1)}, u32[]{:S(2)}, u32[]{:S(2)}) collective-permute-start(f32[1,2,2,16,128]{4,3,2,1,0:T(8,128)S(1)} %get-tuple-element.950), channel_id=1, source_target_pairs={{0,8},{8,16},{16,24},{24,32},{32,40},{40,48},{48,56},{56,64},{64,7... | collective-permute-start | bytes 98312 | tf_op jit(solution)/shard_map/while/body/eval_jaxpr/ppermute | solution.py:16
  51.8 7.9 %collective-permute-start.1 = (f32[1,2,16,2,128]{4,3,2,1,0:T(2,128)S(1)}, f32[1,2,16,2,128]{4,3,2,1,0:T(2,128)S(1)}, u32[]{:S(2)}, u32[]{:S(2)}) collective-permute-start(f32[1,2,16,2,128]{4,3,2,1,0:T(2,128)S(1)} %get-tuple-element.951), channel_id=1, source_target_pairs={{0,1},{1,2},{2,3},{3,4},{4,5},{5,6},{6,7},{8,9},{9,10},{10,11},{11... | collective-permute-start | bytes 98312 | tf_op jit(solution)/shard_map/while/body/eval_jaxpr/ppermute | solution.py:16
  71.2 6.7 %collective-permute-start = (f32[1,2,2,16,128]{4,3,2,1,0:T(8,128)S(1)}, f32[1,2,2,16,128]{4,3,2,1,0:T(8,128)S(1)}, u32[]{:S(2)}, u32[]{:S(2)}) collective-permute-start(f32[1,2,2,16,128]{4,3,2,1,0:T(8,128)S(1)} %get-tuple-element.950), channel_id=1, source_target_pairs={{0,8},{8,16},{16,24},{24,32},{32,40},{40,48},{48,56},{56,64},{64,7... | collective-permute-start | bytes 98312 | tf_op jit(solution)/shard_map/while/body/eval_jaxpr/ppermute | solution.py:16
  74.2 8.0 %collective-permute-start.1 = (f32[1,2,16,2,128]{4,3,2,1,0:T(2,128)S(1)}, f32[1,2,16,2,128]{4,3,2,1,0:T(2,128)S(1)}, u32[]{:S(2)}, u32[]{:S(2)}) collective-permute-start(f32[1,2,16,2,128]{4,3,2,1,0:T(2,128)S(1)} %get-tuple-element.951), channel_id=1, source_target_pairs={{0,1},{1,2},{2,3},{3,4},{4,5},{5,6},{6,7},{8,9},{9,10},{10,11},{11... | collective-permute-start | bytes 98312 | tf_op jit(solution)/shard_map/while/body/eval_jaxpr/ppermute | solution.py:16
  93.6 6.7 %collective-permute-start = (f32[1,2,2,16,128]{4,3,2,1,0:T(8,128)S(1)}, f32[1,2,2,16,128]{4,3,2,1,0:T(8,128)S(1)}, u32[]{:S(2)}, u32[]{:S(2)}) collective-permute-start(f32[1,2,2,16,128]{4,3,2,1,0:T(8,128)S(1)} %get-tuple-element.950), channel_id=1, source_target_pairs={{0,8},{8,16},{16,24},{24,32},{32,40},{40,48},{48,56},{56,64},{64,7... | collective-permute-start | bytes 98312 | tf_op jit(solution)/shard_map/while/body/eval_jaxpr/ppermute | solution.py:16
  95.6 7.9 %collective-permute-start.1 = (f32[1,2,16,2,128]{4,3,2,1,0:T(2,128)S(1)}, f32[1,2,16,2,128]{4,3,2,1,0:T(2,128)S(1)}, u32[]{:S(2)}, u32[]{:S(2)}) collective-permute-start(f32[1,2,16,2,128]{4,3,2,1,0:T(2,128)S(1)} %get-tuple-element.951), channel_id=1, source_target_pairs={{0,1},{1,2},{2,3},{3,4},{4,5},{5,6},{6,7},{8,9},{9,10},{10,11},{11... | collective-permute-start | bytes 98312 | tf_op jit(solution)/shard_map/while/body/eval_jaxpr/ppermute | solution.py:16
  115.0 6.7 %collective-permute-start = (f32[1,2,2,16,128]{4,3,2,1,0:T(8,128)S(1)}, f32[1,2,2,16,128]{4,3,2,1,0:T(8,128)S(1)}, u32[]{:S(2)}, u32[]{:S(2)}) collective-permute-start(f32[1,2,2,16,128]{4,3,2,1,0:T(8,128)S(1)} %get-tuple-element.950), channel_id=1, source_target_pairs={{0,8},{8,16},{16,24},{24,32},{32,40},{40,48},{48,56},{56,64},{64,7... | collective-permute-start | bytes 98312 | tf_op jit(solution)/shard_map/while/body/eval_jaxpr/ppermute | solution.py:16
  118.4 8.0 %collective-permute-start.1 = (f32[1,2,16,2,128]{4,3,2,1,0:T(2,128)S(1)}, f32[1,2,16,2,128]{4,3,2,1,0:T(2,128)S(1)}, u32[]{:S(2)}, u32[]{:S(2)}) collective-permute-start(f32[1,2,16,2,128]{4,3,2,1,0:T(2,128)S(1)} %get-tuple-element.951), channel_id=1, source_target_pairs={{0,1},{1,2},{2,3},{3,4},{4,5},{5,6},{6,7},{8,9},{9,10},{10,11},{11... | collective-permute-start | bytes 98312 | tf_op jit(solution)/shard_map/while/body/eval_jaxpr/ppermute | solution.py:16
  137.8 6.7 %collective-permute-start = (f32[1,2,2,16,128]{4,3,2,1,0:T(8,128)S(1)}, f32[1,2,2,16,128]{4,3,2,1,0:T(8,128)S(1)}, u32[]{:S(2)}, u32[]{:S(2)}) collective-permute-start(f32[1,2,2,16,128]{4,3,2,1,0:T(8,128)S(1)} %get-tuple-element.950), channel_id=1, source_target_pairs={{0,8},{8,16},{16,24},{24,32},{32,40},{40,48},{48,56},{56,64},{64,7... | collective-permute-start | bytes 98312 | tf_op jit(solution)/shard_map/while/body/eval_jaxpr/ppermute | solution.py:16
  139.9 7.9 %collective-permute-start.1 = (f32[1,2,16,2,128]{4,3,2,1,0:T(2,128)S(1)}, f32[1,2,16,2,128]{4,3,2,1,0:T(2,128)S(1)}, u32[]{:S(2)}, u32[]{:S(2)}) collective-permute-start(f32[1,2,16,2,128]{4,3,2,1,0:T(2,128)S(1)} %get-tuple-element.951), channel_id=1, source_target_pairs={{0,1},{1,2},{2,3},{3,4},{4,5},{5,6},{6,7},{8,9},{9,10},{10,11},{11... | collective-permute-start | bytes 98312 | tf_op jit(solution)/shard_map/while/body/eval_jaxpr/ppermute | solution.py:16
  159.2 6.7 %collective-permute-start = (f32[1,2,2,16,128]{4,3,2,1,0:T(8,128)S(1)}, f32[1,2,2,16,128]{4,3,2,1,0:T(8,128)S(1)}, u32[]{:S(2)}, u32[]{:S(2)}) collective-permute-start(f32[1,2,2,16,128]{4,3,2,1,0:T(8,128)S(1)} %get-tuple-element.950), channel_id=1, source_target_pairs={{0,8},{8,16},{16,24},{24,32},{32,40},{40,48},{48,56},{56,64},{64,7... | collective-permute-start | bytes 98312 | tf_op jit(solution)/shard_map/while/body/eval_jaxpr/ppermute | solution.py:16
  162.2 8.0 %collective-permute-start.1 = (f32[1,2,16,2,128]{4,3,2,1,0:T(2,128)S(1)}, f32[1,2,16,2,128]{4,3,2,1,0:T(2,128)S(1)}, u32[]{:S(2)}, u32[]{:S(2)}) collective-permute-start(f32[1,2,16,2,128]{4,3,2,1,0:T(2,128)S(1)} %get-tuple-element.951), channel_id=1, source_target_pairs={{0,1},{1,2},{2,3},{3,4},{4,5},{5,6},{6,7},{8,9},{9,10},{10,11},{11... | collective-permute-start | bytes 98312 | tf_op jit(solution)/shard_map/while/body/eval_jaxpr/ppermute | solution.py:16
  181.6 6.7 %collective-permute-start = (f32[1,2,2,16,128]{4,3,2,1,0:T(8,128)S(1)}, f32[1,2,2,16,128]{4,3,2,1,0:T(8,128)S(1)}, u32[]{:S(2)}, u32[]{:S(2)}) collective-permute-start(f32[1,2,2,16,128]{4,3,2,1,0:T(8,128)S(1)} %get-tuple-element.950), channel_id=1, source_target_pairs={{0,8},{8,16},{16,24},{24,32},{32,40},{40,48},{48,56},{56,64},{64,7... | collective-permute-start | bytes 98312 | tf_op jit(solution)/shard_map/while/body/eval_jaxpr/ppermute | solution.py:16
  183.6 7.9 %collective-permute-start.1 = (f32[1,2,16,2,128]{4,3,2,1,0:T(2,128)S(1)}, f32[1,2,16,2,128]{4,3,2,1,0:T(2,128)S(1)}, u32[]{:S(2)}, u32[]{:S(2)}) collective-permute-start(f32[1,2,16,2,128]{4,3,2,1,0:T(2,128)S(1)} %get-tuple-element.951), channel_id=1, source_target_pairs={{0,1},{1,2},{2,3},{3,4},{4,5},{5,6},{6,7},{8,9},{9,10},{10,11},{11... | collective-permute-start | bytes 98312 | tf_op jit(solution)/shard_map/while/body/eval_jaxpr/ppermute | solution.py:16
  203.0 6.7 %collective-permute-start = (f32[1,2,2,16,128]{4,3,2,1,0:T(8,128)S(1)}, f32[1,2,2,16,128]{4,3,2,1,0:T(8,128)S(1)}, u32[]{:S(2)}, u32[]{:S(2)}) collective-permute-start(f32[1,2,2,16,128]{4,3,2,1,0:T(8,128)S(1)} %get-tuple-element.950), channel_id=1, source_target_pairs={{0,8},{8,16},{16,24},{24,32},{32,40},{40,48},{48,56},{56,64},{64,7... | collective-permute-start | bytes 98312 | tf_op jit(solution)/shard_map/while/body/eval_jaxpr/ppermute | solution.py:16
  206.2 8.0 %collective-permute-start.1 = (f32[1,2,16,2,128]{4,3,2,1,0:T(2,128)S(1)}, f32[1,2,16,2,128]{4,3,2,1,0:T(2,128)S(1)}, u32[]{:S(2)}, u32[]{:S(2)}) collective-permute-start(f32[1,2,16,2,128]{4,3,2,1,0:T(2,128)S(1)} %get-tuple-element.951), channel_id=1, source_target_pairs={{0,1},{1,2},{2,3},{3,4},{4,5},{5,6},{6,7},{8,9},{9,10},{10,11},{11... | collective-permute-start | bytes 98312 | tf_op jit(solution)/shard_map/while/body/eval_jaxpr/ppermute | solution.py:16
  225.6 6.7 %collective-permute-start = (f32[1,2,2,16,128]{4,3,2,1,0:T(8,128)S(1)}, f32[1,2,2,16,128]{4,3,2,1,0:T(8,128)S(1)}, u32[]{:S(2)}, u32[]{:S(2)}) collective-permute-start(f32[1,2,2,16,128]{4,3,2,1,0:T(8,128)S(1)} %get-tuple-element.950), channel_id=1, source_target_pairs={{0,8},{8,16},{16,24},{24,32},{32,40},{40,48},{48,56},{56,64},{64,7... | collective-permute-start | bytes 98312 | tf_op jit(solution)/shard_map/while/body/eval_jaxpr/ppermute | solution.py:16
  227.6 7.9 %collective-permute-start.1 = (f32[1,2,16,2,128]{4,3,2,1,0:T(2,128)S(1)}, f32[1,2,16,2,128]{4,3,2,1,0:T(2,128)S(1)}, u32[]{:S(2)}, u32[]{:S(2)}) collective-permute-start(f32[1,2,16,2,128]{4,3,2,1,0:T(2,128)S(1)} %get-tuple-element.951), channel_id=1, source_target_pairs={{0,1},{1,2},{2,3},{3,4},{4,5},{5,6},{6,7},{8,9},{9,10},{10,11},{11... | collective-permute-start | bytes 98312 | tf_op jit(solution)/shard_map/while/body/eval_jaxpr/ppermute | solution.py:16
  247.0 6.7 %collective-permute-start = (f32[1,2,2,16,128]{4,3,2,1,0:T(8,128)S(1)}, f32[1,2,2,16,128]{4,3,2,1,0:T(8,128)S(1)}, u32[]{:S(2)}, u32[]{:S(2)}) collective-permute-start(f32[1,2,2,16,128]{4,3,2,1,0:T(8,128)S(1)} %get-tuple-element.950), channel_id=1, source_target_pairs={{0,8},{8,16},{16,24},{24,32},{32,40},{40,48},{48,56},{56,64},{64,7... | collective-permute-start | bytes 98312 | tf_op jit(solution)/shard_map/while/body/eval_jaxpr/ppermute | solution.py:16
  249.7 7.9 %collective-permute-start.1 = (f32[1,2,16,2,128]{4,3,2,1,0:T(2,128)S(1)}, f32[1,2,16,2,128]{4,3,2,1,0:T(2,128)S(1)}, u32[]{:S(2)}, u32[]{:S(2)}) collective-permute-start(f32[1,2,16,2,128]{4,3,2,1,0:T(2,128)S(1)} %get-tuple-element.951), channel_id=1, source_target_pairs={{0,1},{1,2},{2,3},{3,4},{4,5},{5,6},{6,7},{8,9},{9,10},{10,11},{11... | collective-permute-start | bytes 98312 | tf_op jit(solution)/shard_map/while/body/eval_jaxpr/ppermute | solution.py:16
  269.1 6.7 %collective-permute-start = (f32[1,2,2,16,128]{4,3,2,1,0:T(8,128)S(1)}, f32[1,2,2,16,128]{4,3,2,1,0:T(8,128)S(1)}, u32[]{:S(2)}, u32[]{:S(2)}) collective-permute-start(f32[1,2,2,16,128]{4,3,2,1,0:T(8,128)S(1)} %get-tuple-element.950), channel_id=1, source_target_pairs={{0,8},{8,16},{16,24},{24,32},{32,40},{40,48},{48,56},{56,64},{64,7... | collective-permute-start | bytes 98312 | tf_op jit(solution)/shard_map/while/body/eval_jaxpr/ppermute | solution.py:16
  271.4 7.9 %collective-permute-start.1 = (f32[1,2,16,2,128]{4,3,2,1,0:T(2,128)S(1)}, f32[1,2,16,2,128]{4,3,2,1,0:T(2,128)S(1)}, u32[]{:S(2)}, u32[]{:S(2)}) collective-permute-start(f32[1,2,16,2,128]{4,3,2,1,0:T(2,128)S(1)} %get-tuple-element.951), channel_id=1, source_target_pairs={{0,1},{1,2},{2,3},{3,4},{4,5},{5,6},{6,7},{8,9},{9,10},{10,11},{11... | collective-permute-start | bytes 98312 | tf_op jit(solution)/shard_map/while/body/eval_jaxpr/ppermute | solution.py:16
  290.8 6.7 %collective-permute-start = (f32[1,2,2,16,128]{4,3,2,1,0:T(8,128)S(1)}, f32[1,2,2,16,128]{4,3,2,1,0:T(8,128)S(1)}, u32[]{:S(2)}, u32[]{:S(2)}) collective-permute-start(f32[1,2,2,16,128]{4,3,2,1,0:T(8,128)S(1)} %get-tuple-element.950), channel_id=1, source_target_pairs={{0,8},{8,16},{16,24},{24,32},{32,40},{40,48},{48,56},{56,64},{64,7... | collective-permute-start | bytes 98312 | tf_op jit(solution)/shard_map/while/body/eval_jaxpr/ppermute | solution.py:16
  293.3 7.9 %collective-permute-start.1 = (f32[1,2,16,2,128]{4,3,2,1,0:T(2,128)S(1)}, f32[1,2,16,2,128]{4,3,2,1,0:T(2,128)S(1)}, u32[]{:S(2)}, u32[]{:S(2)}) collective-permute-start(f32[1,2,16,2,128]{4,3,2,1,0:T(2,128)S(1)} %get-tuple-element.951), channel_id=1, source_target_pairs={{0,1},{1,2},{2,3},{3,4},{4,5},{5,6},{6,7},{8,9},{9,10},{10,11},{11... | collective-permute-start | bytes 98312 | tf_op jit(solution)/shard_map/while/body/eval_jaxpr/ppermute | solution.py:16
  312.6 6.7 %collective-permute-start = (f32[1,2,2,16,128]{4,3,2,1,0:T(8,128)S(1)}, f32[1,2,2,16,128]{4,3,2,1,0:T(8,128)S(1)}, u32[]{:S(2)}, u32[]{:S(2)}) collective-permute-start(f32[1,2,2,16,128]{4,3,2,1,0:T(8,128)S(1)} %get-tuple-element.950), channel_id=1, source_target_pairs={{0,8},{8,16},{16,24},{24,32},{32,40},{40,48},{48,56},{56,64},{64,7... | collective-permute-start | bytes 98312 | tf_op jit(solution)/shard_map/while/body/eval_jaxpr/ppermute | solution.py:16
  315.1 7.9 %collective-permute-start.1 = (f32[1,2,16,2,128]{4,3,2,1,0:T(2,128)S(1)}, f32[1,2,16,2,128]{4,3,2,1,0:T(2,128)S(1)}, u32[]{:S(2)}, u32[]{:S(2)}) collective-permute-start(f32[1,2,16,2,128]{4,3,2,1,0:T(2,128)S(1)} %get-tuple-element.951), channel_id=1, source_target_pairs={{0,1},{1,2},{2,3},{3,4},{4,5},{5,6},{6,7},{8,9},{9,10},{10,11},{11... | collective-permute-start | bytes 98312 | tf_op jit(solution)/shard_map/while/body/eval_jaxpr/ppermute | solution.py:16
  334.4 6.7 %collective-permute-start = (f32[1,2,2,16,128]{4,3,2,1,0:T(8,128)S(1)}, f32[1,2,2,16,128]{4,3,2,1,0:T(8,128)S(1)}, u32[]{:S(2)}, u32[]{:S(2)}) collective-permute-start(f32[1,2,2,16,128]{4,3,2,1,0:T(8,128)S(1)} %get-tuple-element.950), channel_id=1, source_target_pairs={{0,8},{8,16},{16,24},{24,32},{32,40},{40,48},{48,56},{56,64},{64,7... | collective-permute-start | bytes 98312 | tf_op jit(solution)/shard_map/while/body/eval_jaxpr/ppermute | solution.py:16
  336.7 7.9 %collective-permute-start.1 = (f32[1,2,16,2,128]{4,3,2,1,0:T(2,128)S(1)}, f32[1,2,16,2,128]{4,3,2,1,0:T(2,128)S(1)}, u32[]{:S(2)}, u32[]{:S(2)}) collective-permute-start(f32[1,2,16,2,128]{4,3,2,1,0:T(2,128)S(1)} %get-tuple-element.951), channel_id=1, source_target_pairs={{0,1},{1,2},{2,3},{3,4},{4,5},{5,6},{6,7},{8,9},{9,10},{10,11},{11... | collective-permute-start | bytes 98312 | tf_op jit(solution)/shard_map/while/body/eval_jaxpr/ppermute | solution.py:16
  356.0 6.7 %collective-permute-start = (f32[1,2,2,16,128]{4,3,2,1,0:T(8,128)S(1)}, f32[1,2,2,16,128]{4,3,2,1,0:T(8,128)S(1)}, u32[]{:S(2)}, u32[]{:S(2)}) collective-permute-start(f32[1,2,2,16,128]{4,3,2,1,0:T(8,128)S(1)} %get-tuple-element.950), channel_id=1, source_target_pairs={{0,8},{8,16},{16,24},{24,32},{32,40},{40,48},{48,56},{56,64},{64,7... | collective-permute-start | bytes 98312 | tf_op jit(solution)/shard_map/while/body/eval_jaxpr/ppermute | solution.py:16
  358.4 7.9 %collective-permute-start.1 = (f32[1,2,16,2,128]{4,3,2,1,0:T(2,128)S(1)}, f32[1,2,16,2,128]{4,3,2,1,0:T(2,128)S(1)}, u32[]{:S(2)}, u32[]{:S(2)}) collective-permute-start(f32[1,2,16,2,128]{4,3,2,1,0:T(2,128)S(1)} %get-tuple-element.951), channel_id=1, source_target_pairs={{0,1},{1,2},{2,3},{3,4},{4,5},{5,6},{6,7},{8,9},{9,10},{10,11},{11... | collective-permute-start | bytes 98312 | tf_op jit(solution)/shard_map/while/body/eval_jaxpr/ppermute | solution.py:16
  377.7 6.7 %collective-permute-start = (f32[1,2,2,16,128]{4,3,2,1,0:T(8,128)S(1)}, f32[1,2,2,16,128]{4,3,2,1,0:T(8,128)S(1)}, u32[]{:S(2)}, u32[]{:S(2)}) collective-permute-start(f32[1,2,2,16,128]{4,3,2,1,0:T(8,128)S(1)} %get-tuple-element.950), channel_id=1, source_target_pairs={{0,8},{8,16},{16,24},{24,32},{32,40},{40,48},{48,56},{56,64},{64,7... | collective-permute-start | bytes 98312 | tf_op jit(solution)/shard_map/while/body/eval_jaxpr/ppermute | solution.py:16
  380.0 8.0 %collective-permute-start.1 = (f32[1,2,16,2,128]{4,3,2,1,0:T(2,128)S(1)}, f32[1,2,16,2,128]{4,3,2,1,0:T(2,128)S(1)}, u32[]{:S(2)}, u32[]{:S(2)}) collective-permute-start(f32[1,2,16,2,128]{4,3,2,1,0:T(2,128)S(1)} %get-tuple-element.951), channel_id=1, source_target_pairs={{0,1},{1,2},{2,3},{3,4},{4,5},{5,6},{6,7},{8,9},{9,10},{10,11},{11... | collective-permute-start | bytes 98312 | tf_op jit(solution)/shard_map/while/body/eval_jaxpr/ppermute | solution.py:16
  399.5 6.7 %collective-permute-start = (f32[1,2,2,16,128]{4,3,2,1,0:T(8,128)S(1)}, f32[1,2,2,16,128]{4,3,2,1,0:T(8,128)S(1)}, u32[]{:S(2)}, u32[]{:S(2)}) collective-permute-start(f32[1,2,2,16,128]{4,3,2,1,0:T(8,128)S(1)} %get-tuple-element.950), channel_id=1, source_target_pairs={{0,8},{8,16},{16,24},{24,32},{32,40},{40,48},{48,56},{56,64},{64,7... | collective-permute-start | bytes 98312 | tf_op jit(solution)/shard_map/while/body/eval_jaxpr/ppermute | solution.py:16
  401.6 8.3 %collective-permute-start.1 = (f32[1,2,16,2,128]{4,3,2,1,0:T(2,128)S(1)}, f32[1,2,16,2,128]{4,3,2,1,0:T(2,128)S(1)}, u32[]{:S(2)}, u32[]{:S(2)}) collective-permute-start(f32[1,2,16,2,128]{4,3,2,1,0:T(2,128)S(1)} %get-tuple-element.951), channel_id=1, source_target_pairs={{0,1},{1,2},{2,3},{3,4},{4,5},{5,6},{6,7},{8,9},{9,10},{10,11},{11... | collective-permute-start | bytes 98312 | tf_op jit(solution)/shard_map/while/body/eval_jaxpr/ppermute | solution.py:16
  421.2 6.7 %collective-permute-start = (f32[1,2,2,16,128]{4,3,2,1,0:T(8,128)S(1)}, f32[1,2,2,16,128]{4,3,2,1,0:T(8,128)S(1)}, u32[]{:S(2)}, u32[]{:S(2)}) collective-permute-start(f32[1,2,2,16,128]{4,3,2,1,0:T(8,128)S(1)} %get-tuple-element.950), channel_id=1, source_target_pairs={{0,8},{8,16},{16,24},{24,32},{32,40},{40,48},{48,56},{56,64},{64,7... | collective-permute-start | bytes 98312 | tf_op jit(solution)/shard_map/while/body/eval_jaxpr/ppermute | solution.py:16
  423.3 7.9 %collective-permute-start.1 = (f32[1,2,16,2,128]{4,3,2,1,0:T(2,128)S(1)}, f32[1,2,16,2,128]{4,3,2,1,0:T(2,128)S(1)}, u32[]{:S(2)}, u32[]{:S(2)}) collective-permute-start(f32[1,2,16,2,128]{4,3,2,1,0:T(2,128)S(1)} %get-tuple-element.951), channel_id=1, source_target_pairs={{0,1},{1,2},{2,3},{3,4},{4,5},{5,6},{6,7},{8,9},{9,10},{10,11},{11... | collective-permute-start | bytes 98312 | tf_op jit(solution)/shard_map/while/body/eval_jaxpr/ppermute | solution.py:16
  442.6 6.7 %collective-permute-start = (f32[1,2,2,16,128]{4,3,2,1,0:T(8,128)S(1)}, f32[1,2,2,16,128]{4,3,2,1,0:T(8,128)S(1)}, u32[]{:S(2)}, u32[]{:S(2)}) collective-permute-start(f32[1,2,2,16,128]{4,3,2,1,0:T(8,128)S(1)} %get-tuple-element.950), channel_id=1, source_target_pairs={{0,8},{8,16},{16,24},{24,32},{32,40},{40,48},{48,56},{56,64},{64,7... | collective-permute-start | bytes 98312 | tf_op jit(solution)/shard_map/while/body/eval_jaxpr/ppermute | solution.py:16
  444.6 7.9 %collective-permute-start.1 = (f32[1,2,16,2,128]{4,3,2,1,0:T(2,128)S(1)}, f32[1,2,16,2,128]{4,3,2,1,0:T(2,128)S(1)}, u32[]{:S(2)}, u32[]{:S(2)}) collective-permute-start(f32[1,2,16,2,128]{4,3,2,1,0:T(2,128)S(1)} %get-tuple-element.951), channel_id=1, source_target_pairs={{0,1},{1,2},{2,3},{3,4},{4,5},{5,6},{6,7},{8,9},{9,10},{10,11},{11... | collective-permute-start | bytes 98312 | tf_op jit(solution)/shard_map/while/body/eval_jaxpr/ppermute | solution.py:16
  463.9 6.7 %collective-permute-start = (f32[1,2,2,16,128]{4,3,2,1,0:T(8,128)S(1)}, f32[1,2,2,16,128]{4,3,2,1,0:T(8,128)S(1)}, u32[]{:S(2)}, u32[]{:S(2)}) collective-permute-start(f32[1,2,2,16,128]{4,3,2,1,0:T(8,128)S(1)} %get-tuple-element.950), channel_id=1, source_target_pairs={{0,8},{8,16},{16,24},{24,32},{32,40},{40,48},{48,56},{56,64},{64,7... | collective-permute-start | bytes 98312 | tf_op jit(solution)/shard_map/while/body/eval_jaxpr/ppermute | solution.py:16
  465.9 7.9 %collective-permute-start.1 = (f32[1,2,16,2,128]{4,3,2,1,0:T(2,128)S(1)}, f32[1,2,16,2,128]{4,3,2,1,0:T(2,128)S(1)}, u32[]{:S(2)}, u32[]{:S(2)}) collective-permute-start(f32[1,2,16,2,128]{4,3,2,1,0:T(2,128)S(1)} %get-tuple-element.951), channel_id=1, source_target_pairs={{0,1},{1,2},{2,3},{3,4},{4,5},{5,6},{6,7},{8,9},{9,10},{10,11},{11... | collective-permute-start | bytes 98312 | tf_op jit(solution)/shard_map/while/body/eval_jaxpr/ppermute | solution.py:16
  485.2 6.7 %collective-permute-start = (f32[1,2,2,16,128]{4,3,2,1,0:T(8,128)S(1)}, f32[1,2,2,16,128]{4,3,2,1,0:T(8,128)S(1)}, u32[]{:S(2)}, u32[]{:S(2)}) collective-permute-start(f32[1,2,2,16,128]{4,3,2,1,0:T(8,128)S(1)} %get-tuple-element.950), channel_id=1, source_target_pairs={{0,8},{8,16},{16,24},{24,32},{32,40},{40,48},{48,56},{56,64},{64,7... | collective-permute-start | bytes 98312 | tf_op jit(solution)/shard_map/while/body/eval_jaxpr/ppermute | solution.py:16
  487.1 7.9 %collective-permute-start.1 = (f32[1,2,16,2,128]{4,3,2,1,0:T(2,128)S(1)}, f32[1,2,16,2,128]{4,3,2,1,0:T(2,128)S(1)}, u32[]{:S(2)}, u32[]{:S(2)}) collective-permute-start(f32[1,2,16,2,128]{4,3,2,1,0:T(2,128)S(1)} %get-tuple-element.951), channel_id=1, source_target_pairs={{0,1},{1,2},{2,3},{3,4},{4,5},{5,6},{6,7},{8,9},{9,10},{10,11},{11... | collective-permute-start | bytes 98312 | tf_op jit(solution)/shard_map/while/body/eval_jaxpr/ppermute | solution.py:16
  506.5 6.7 %collective-permute-start = (f32[1,2,2,16,128]{4,3,2,1,0:T(8,128)S(1)}, f32[1,2,2,16,128]{4,3,2,1,0:T(8,128)S(1)}, u32[]{:S(2)}, u32[]{:S(2)}) collective-permute-start(f32[1,2,2,16,128]{4,3,2,1,0:T(8,128)S(1)} %get-tuple-element.950), channel_id=1, source_target_pairs={{0,8},{8,16},{16,24},{24,32},{32,40},{40,48},{48,56},{56,64},{64,7... | collective-permute-start | bytes 98312 | tf_op jit(solution)/shard_map/while/body/eval_jaxpr/ppermute | solution.py:16
  508.4 7.9 %collective-permute-start.1 = (f32[1,2,16,2,128]{4,3,2,1,0:T(2,128)S(1)}, f32[1,2,16,2,128]{4,3,2,1,0:T(2,128)S(1)}, u32[]{:S(2)}, u32[]{:S(2)}) collective-permute-start(f32[1,2,16,2,128]{4,3,2,1,0:T(2,128)S(1)} %get-tuple-element.951), channel_id=1, source_target_pairs={{0,1},{1,2},{2,3},{3,4},{4,5},{5,6},{6,7},{8,9},{9,10},{10,11},{11... | collective-permute-start | bytes 98312 | tf_op jit(solution)/shard_map/while/body/eval_jaxpr/ppermute | solution.py:16
  (6 other events, 15.6 us)
where the time goes:
time: 544 us; the launch traced here: 541 us
  matrix products  233 us (43%)
  waiting for transfers between devices  144 us (26%)
  starting transfers between devices  111 us (20%)
  other arithmetic  31.1 us (6%)
  local copies, waits for them, and re-layouts  11.7 us (2%)
  loops' own time  9.17 us (2%)
    ppermute x50, waiting for transfers between devices, passed_along(): return lax.ppermute(array, axis, pairs)  144 us
    ppermute x50, starting transfers between devices, passed_along(): return lax.ppermute(array, axis, pairs)  111 us
    dot_general x144, matrix products, transform(): result = jnp.einsum('scxyz,zw->scxyw', wavefield, sine_z, precision=HIGHEST)  94.9 us
    dot_general x144, matrix products, transform(): return jnp.einsum('scxyz,yb->scxbz', result, sine_y, precision=HIGHEST)  70.4 us
    dot_general x144, matrix products, transform(): result = jnp.einsum('scxyz,xa->scayz', result, sine_x, precision=HIGHEST)  66.4 us
    sub x49, other arithmetic, apply_operator(): lateral = lateral + 2.0 * center - vertical[..., :-2] - vertical[..., 2:]  12.5 us
  transfers between devices with their start and end apart: 50, of which 49 were waited for; matrix products, arithmetic and copies ran while one was open for 0% of the time, Pallas kernels for 0%

commit v1 on v0

v1 whole, which is shorter than its diff:
```python
import functools

import jax
import jax.numpy as jnp
import numpy as np
from jax import lax
from jax.experimental import pallas as pl
from jax.experimental.pallas import tpu as pltpu
from jax.sharding import PartitionSpec as P

KAPPA = 0.12
DAMPING = 0.3
MESH = pl.DeviceIdType.MESH
F32 = jnp.float32
BF16 = jnp.bfloat16


def split_table(table):
    high = np.asarray(table, np.float32).astype(BF16)
    low = (np.asarray(table, np.float64) - high.astype(np.float64)).astype(np.float32).astype(BF16)
    return high, low


def stacked(table):
    high, low = split_table(table)
    return np.concatenate([high, low, high], axis=1)


def sine_basis(length):
    positions = np.arange(1, length + 1, dtype=np.float64)
    angles = positions * (np.pi / (length + 1))
    return np.sqrt(2.0 / (length + 1)) * np.sin(angles[:, None] * positions[None, :]), angles


def build_tables(size_x, size_y, cells_z):
    sine_x, angle_x = sine_basis(size_x)
    sine_y, angle_y = sine_basis(size_y)
    sine_z, angle_z = sine_basis(cells_z)
    symbol_x = 2.5 - 8.0 / 3.0 * np.cos(angle_x) + np.cos(2.0 * angle_x) / 6.0
    symbol_y = 2.5 - 8.0 / 3.0 * np.cos(angle_y) + np.cos(2.0 * angle_y) / 6.0
    symbol_z = 2.0 - 2.0 * np.cos(angle_z)
    real_part = symbol_x[:, None, None] + symbol_y[None, :, None] + symbol_z - KAPPA
    denominator = real_part * real_part + (KAPPA * DAMPING) ** 2
    inverse_real = (real_part / denominator).reshape(size_x * size_y, cells_z).astype(np.float32)
    inverse_imag = (KAPPA * DAMPING / denominator).reshape(size_x * size_y, cells_z)
    inverse_imag = inverse_imag.astype(np.float32)
    horizontal = stacked(np.kron(sine_x, sine_y))
    high, low = split_table(sine_z)
    vertical = np.concatenate([np.concatenate([high, low], axis=1)] * 2, axis=0)
    eye_x = np.eye(size_x)
    eye_y = np.eye(size_y)

    def inward(sine):
        return (-sine[:, 0] / 12.0, (16.0 * sine[:, 0] - sine[:, 1]) / 12.0)

    spread = [np.kron(v[:, None], eye_y) for v in inward(sine_x)]
    spread += [np.kron(eye_x, v[:, None]) for v in inward(sine_y)]
    gather = [np.kron(sine_x[size_x - 2 + l][None, :], eye_y) for l in range(2)]
    gather += [np.kron(eye_x, sine_y[size_y - 2 + l][None, :]) for l in range(2)]
    edge_x = np.zeros(size_x)
    edge_x[[0, -1]] = 1.0 / 12.0
    edge_y = np.zeros(size_y)
    edge_y[[0, -1]] = 1.0 / 12.0
    edges = np.repeat((edge_x[:, None] + edge_y[None, :]).reshape(-1, 1), cells_z, axis=1)
    return (
        horizontal,
        vertical,
        stacked(np.concatenate(spread, axis=1)),
        stacked(np.concatenate(gather, axis=0)),
        inverse_real,
        inverse_imag,
        edges.astype(np.float32),
    )


def split(values):
    high = values.astype(BF16)
    return high, (values - high.astype(F32)).astype(BF16)


def product(table, values):
    high, low = split(values)
    return jnp.dot(
        table, jnp.concatenate([high, high, low], axis=0), preferred_element_type=F32
    )


def along_z(values, vertical):
    half = values.shape[1] // 2
    high, low = split(values)
    outs = []
    for part in range(2):
        lanes = slice(part * half, (part + 1) * half)
        both = jnp.concatenate([high[:, lanes], low[:, lanes]], axis=1)
        mixed = jnp.dot(both, vertical, preferred_element_type=F32)
        outs.append(mixed[:, :half] + mixed[:, half:])
    return jnp.concatenate(outs, axis=1)


def times(real, imag, values):
    half = values.shape[1] // 2
    first, second = values[:, :half], values[:, half:]
    return jnp.concatenate(
        [real * first - imag * second, real * second + imag * first], axis=1
    )


def kernel(
    grid_rows, grid_cols, cells,
    rs_ref, slow_ref, cells_ref, amp_ref,
    hor_ref, ver_ref, spread_ref, gather_ref, lam_r, lam_i, edge_ref,
    wave_ref, resid_ref,
    fhat, spec, inner, inbound, outbound, back_x, back_y, after_x, after_y,
    send_sem, recv_sem, back_send, back_recv,
):
    size_x, size_y, size_z = cells
    rows = size_x * size_y
    count = rs_ref.shape[0]
    row = lax.axis_index("gx")
    col = lax.axis_index("gy")
    has_prev = (row > 0, col > 0)
    has_next = (row < grid_rows - 1, col < grid_cols - 1)
    nexts = ({"gx": row + 1}, {"gy": col + 1})
    prevs = ({"gx": row - 1}, {"gy": col - 1})
    barrier = pltpu.get_barrier_semaphore()
    for axis in range(2):
        @pl.when(has_prev[axis])
        def _():
            pl.semaphore_signal(barrier, inc=1, device_id=prevs[axis], device_id_type=MESH)

        @pl.when(has_next[axis])
        def _():
            pl.semaphore_signal(barrier, inc=1, device_id=nexts[axis], device_id_type=MESH)

    def forward(values):
        return product(hor_ref[...], along_z(values, ver_ref[...]))

    def medium():
        contrast = slow_ref[...] - 1.0
        return KAPPA * contrast - edge_ref[...], (KAPPA * DAMPING) * contrast

    def modes(values):
        return times(lam_r[...], lam_i[...], values)

    row_ids = lax.broadcasted_iota(jnp.int32, (rows, size_z), 0)
    lane_ids = lax.broadcasted_iota(jnp.int32, (rows, size_z), 1)
    cell_x = row_ids // size_y + row * size_x
    cell_y = row_ids % size_y + col * size_y
    flat = (cell_x * (size_y * grid_cols) + cell_y) * size_z + lane_ids

    def forcing(s):
        real = rs_ref[s, 0]
        imag = rs_ref[s, 1]
        for p in range(cells_ref.shape[1]):
            hit = flat == cells_ref[s, p]
            real = real + jnp.where(hit, amp_ref[s, 2 * p], 0.0)
            imag = imag + jnp.where(hit, amp_ref[s, 2 * p + 1], 0.0)
        return jnp.concatenate([real, imag], axis=1)

    def prepare(s, _):
        fhat[s] = forward(forcing(s))
        return 0

    lax.fori_loop(0, count, prepare, 0)
    for axis in range(2):
        @pl.when(jnp.logical_not(has_prev[axis]))
        def _():
            inbound[:, axis] = jnp.zeros_like(inbound[:, axis])

    peers = sum(flag.astype(jnp.int32) for flag in has_prev + has_next)
    pl.semaphore_wait(barrier, peers)

    def onward(s, axis):
        return pltpu.make_async_remote_copy(
            src_ref=outbound.at[s, axis],
            dst_ref=inbound.at[s, axis],
            send_sem=send_sem.at[s, axis],
            recv_sem=recv_sem.at[s, axis],
            device_id=nexts[axis],
            device_id_type=MESH,
        )

    def backward(s, axis):
        source, target = ((back_x, after_x), (back_y, after_y))[axis]
        return pltpu.make_async_remote_copy(
            src_ref=source.at[s],
            dst_ref=target.at[s],
            send_sem=back_send.at[s, axis],
            recv_sem=back_recv.at[s, axis],
            device_id=prevs[axis],
            device_id_type=MESH,
        )

    def chain(s, _):
        for axis in range(2):
            @pl.when(has_prev[axis])
            def _():
                onward(s, axis).wait_recv()
        traces = jnp.concatenate([inbound[s, 0], inbound[s, 1]], axis=0)
        ghat = fhat[s] + product(spread_ref[...], traces)
        fhat[s] = ghat
        spec[s] = modes(ghat)
        for sweep in range(2):
            real, imag = medium()
            physical = times(real, imag, forward(spec[s]))
            inner[s] = physical
            spec[s] = modes(fhat[s] + forward(physical))
        out = product(gather_ref[...], spec[s])
        half = 2 * size_y
        outbound[s, 0] = out[:half]
        outbound[s, 1] = out[half:]
        for axis in range(2):
            @pl.when(has_next[axis])
            def _():
                onward(s, axis).start()
        return 0

    lax.fori_loop(0, count, chain, 0)

    def finish(s, _):
        wave = forward(spec[s])
        spec[s] = wave
        back_x[s] = wave[: 2 * size_y]
        real, imag = medium()
        inner[s] = times(real, imag, wave) - inner[s]
        wave_ref[s, 0] = wave[:, :size_z]
        wave_ref[s, 1] = wave[:, size_z:]
        for l in range(2):
            for c in range(2):
                back_y[s, l, :, c * size_z : (c + 1) * size_z] = wave_ref[
                    s, c, pl.ds(l, size_x, stride=size_y), :
                ]
        for axis in range(2):
            @pl.when(has_prev[axis])
            def _():
                backward(s, axis).start()
        return 0

    lax.fori_loop(0, count, finish, 0)

    def close(s, _):
        for c in range(2):
            resid_ref[s, c] = inner[s, :, c * size_z : (c + 1) * size_z]

        @pl.when(has_next[0])
        def _():
            backward(s, 0).wait_recv()
            near = after_x[s, :size_y]
            far = after_x[s, size_y:]
            for c in range(2):
                lanes = slice(c * size_z, (c + 1) * size_z)
                resid_ref[s, c, rows - 2 * size_y : rows - size_y] -= near[:, lanes] / 12.0
                resid_ref[s, c, rows - size_y :] += (16.0 * near - far)[:, lanes] / 12.0

        @pl.when(has_next[1])
        def _():
            backward(s, 1).wait_recv()
            near = after_y[s, 0]
            far = after_y[s, 1]
            for c in range(2):
                lanes = slice(c * size_z, (c + 1) * size_z)
                below = pl.ds(size_y - 2, size_x, stride=size_y)
                last = pl.ds(size_y - 1, size_x, stride=size_y)
                resid_ref[s, c, below, :] = resid_ref[s, c, below, :] - near[:, lanes] / 12.0
                resid_ref[s, c, last, :] = (
                    resid_ref[s, c, last, :] + (16.0 * near - far)[:, lanes] / 12.0
                )
        for axis in range(2):
            @pl.when(has_next[axis])
            def _():
                onward(s, axis).wait_send()

            @pl.when(has_prev[axis])
            def _():
                backward(s, axis).wait_send()
        return 0

    lax.fori_loop(0, count, close, 0)


def solution(mesh):
    grid_rows, grid_cols = mesh.shape["gx"], mesh.shape["gy"]

    def body(right_side, slowness, source_cells, source_amplitudes):
        count, parts, size_x, size_y, size_z = right_side.shape
        rows = size_x * size_y
        wide = 2 * size_z
        tables = build_tables(size_x, size_y, size_z)
        full = pl.BlockSpec(memory_space=pltpu.VMEM)
        scalars = pl.BlockSpec(memory_space=pltpu.SMEM)
        block = jax.ShapeDtypeStruct((count, parts, rows, size_z), F32)
        wave, resid = pl.pallas_call(
            functools.partial(kernel, grid_rows, grid_cols, (size_x, size_y, size_z)),
            out_shape=(block, block),
            in_specs=[full, full, scalars, scalars] + [full] * len(tables),
            out_specs=(full, full),
            scratch_shapes=[
                pltpu.VMEM((count, rows, wide), F32),
                pltpu.VMEM((count, rows, wide), F32),
                pltpu.VMEM((count, rows, wide), F32),
                pltpu.VMEM((count, 2, 2 * size_y, wide), F32),
                pltpu.VMEM((count, 2, 2 * size_y, wide), F32),
                pltpu.VMEM((count, 2 * size_y, wide), F32),
                pltpu.VMEM((count, 2, size_x, wide), F32),
                pltpu.VMEM((count, 2 * size_y, wide), F32),
                pltpu.VMEM((count, 2, size_x, wide), F32),
                pltpu.SemaphoreType.DMA((count, 2)),
                pltpu.SemaphoreType.DMA((count, 2)),
                pltpu.SemaphoreType.DMA((count, 2)),
                pltpu.SemaphoreType.DMA((count, 2)),
            ],
            compiler_params=pltpu.CompilerParams(collective_id=0, has_side_effects=True),
        )(
            right_side.reshape(count, parts, rows, size_z),
            slowness.reshape(rows, size_z),
            source_cells,
            source_amplitudes.reshape(count, -1),
            *[jnp.asarray(t) for t in tables],
        )
        shape = (count, parts, size_x, size_y, size_z)
        return (wave.reshape(shape), resid.reshape(shape))

    return jax.shard_map(
        body,
        mesh=mesh,
        in_specs=(P(None, None, "gx", "gy", None), P("gx", "gy", None), P(), P()),
        out_specs=(P(None, None, "gx", "gy", None), P(None, None, "gx", "gy", None)),
        check_vma=False,
    )
```

time: 544 us -> 121 us (0.22)
  the two profiles are of different devices: /device:TPU:6 before, /device:TPU:119 now
where the time goes in v1:
time: 121 us
  Pallas kernels  116 us (96%)
  local copies, waits for them, and re-layouts  4.14 us (3%)
    pallas_call x1, Pallas kernels, body(): pl.pallas_call(functools.partial(kernel, grid_rows, grid_cols, (size_x, s...  116 us
    unnamed x7, local copies, waits for them, and re-layouts  3.49 us

profile of v1, /device:TPU:119, one launch (start us, length us, event | category | flops | bytes accessed | tf_op | source)
XLA Modules:
  0.0 121.3 jit_solution(11599945478980923649)
XLA Ops:
  0.6 0.0 copy-start.1
  0.6 0.7 copy-done.1
  1.3 0.1 copy.14
  1.4 0.7 reshape.21.amp_ref
  2.1 116.5 %shard_map.122 = (f32[2,2,256,128]{3,2,1,0:T(8,128)}, f32[2,2,256,128]{3,2,1,0:T(8,128)}) custom-call(f32[2,2,256,128]{3,2,1,0:T(8,128)} %bitcast.6, f32[256,128]{1,0:T(8,128)} %bitcast.7, s32[2,16]{1,0:T(2,128)} %cells_ref.1, f32[2,32]{1,0:T(2,128)} %reshape.21.amp_ref, bf16[256,768]{1,0:T(8,128)(2,1)} %constant.14.clone.hor_ref, ...), custom_call_target="tpu_custom_call" | custom-call | tf_op jit(solution)/shard_map/pallas_call | solution.py:292
  118.6 0.0 copy-start
  118.6 1.9 %copy.17 = f32[2,2,16,16,128]{4,3,2,1,0:T(8,128)} copy(f32[2,2,16,16,128]{4,3,2,1,0:T(8,128)} %bitcast.5) | data formatting | bytes 1048576
  120.5 0.0 copy-done
  120.5 0.8 copy.18
Async XLA Ops:
  0.6 0.7 copy-start.1
  118.6 1.9 %copy-start = (f32[2,2,256,128]{3,2,1,0:T(8,128)S(1)}, f32[2,2,256,128]{3,2,1,0:T(8,128)}, u32[]{:S(2)}) copy-start(f32[2,2,256,128]{3,2,1,0:T(8,128)} %get-tuple-element.5) | copy-start | bytes 1572868

commit v2 on v1

v2 whole, which is shorter than its diff:
```python
import functools

import jax
import jax.numpy as jnp
import numpy as np
from jax import lax
from jax.experimental import pallas as pl
from jax.experimental.pallas import tpu as pltpu
from jax.sharding import PartitionSpec as P

KAPPA = 0.12
DAMPING = 0.3
MESH = pl.DeviceIdType.MESH
F32 = jnp.float32
BF16 = jnp.bfloat16


def split_table(table):
    high = np.asarray(table, np.float32).astype(BF16)
    low = (np.asarray(table, np.float64) - high.astype(np.float64)).astype(np.float32).astype(BF16)
    return high, low


def stacked(table):
    high, low = split_table(table)
    return np.concatenate([high, low, high], axis=1)


def sine_basis(length):
    positions = np.arange(1, length + 1, dtype=np.float64)
    angles = positions * (np.pi / (length + 1))
    return np.sqrt(2.0 / (length + 1)) * np.sin(angles[:, None] * positions[None, :]), angles


def build_tables(size_x, size_y, cells_z):
    sine_x, angle_x = sine_basis(size_x)
    sine_y, angle_y = sine_basis(size_y)
    sine_z, angle_z = sine_basis(cells_z)
    symbol_x = 2.5 - 8.0 / 3.0 * np.cos(angle_x) + np.cos(2.0 * angle_x) / 6.0
    symbol_y = 2.5 - 8.0 / 3.0 * np.cos(angle_y) + np.cos(2.0 * angle_y) / 6.0
    symbol_z = 2.0 - 2.0 * np.cos(angle_z)
    real_part = symbol_x[:, None, None] + symbol_y[None, :, None] + symbol_z - KAPPA
    denominator = real_part * real_part + (KAPPA * DAMPING) ** 2
    inverse_real = (real_part / denominator).reshape(size_x * size_y, cells_z).astype(np.float32)
    inverse_imag = (KAPPA * DAMPING / denominator).reshape(size_x * size_y, cells_z)
    inverse_imag = inverse_imag.astype(np.float32)
    half_x, half_y = size_x // 2, size_y // 2
    order = np.arange(size_x * size_y).reshape(half_x, 2, half_y, 2)
    order = order.transpose(1, 3, 0, 2).reshape(-1)
    folded = np.arange(size_x * size_y).reshape(size_x, 2, half_y)
    folded[:, 1] = folded[:, 1, ::-1]
    folded = folded.reshape(-1)
    blocks = [
        np.kron(sine_x[:half_x, a::2], sine_y[:half_y, b::2]) for a in range(2) for b in range(2)
    ]
    outward = np.stack([stacked(block) for block in blocks])
    inverse = np.stack([stacked(block.T) for block in blocks])
    horizontal = stacked(np.kron(sine_x, sine_y)[order])
    high, low = split_table(sine_z)
    vertical = np.concatenate([np.concatenate([high, low], axis=1)] * 2, axis=0)
    eye_x = np.eye(size_x)
    eye_y = np.eye(size_y)

    def inward(sine):
        return (-sine[:, 0] / 12.0, (16.0 * sine[:, 0] - sine[:, 1]) / 12.0)

    spread = [np.kron(v[:, None], eye_y) for v in inward(sine_x)]
    spread += [np.kron(eye_x, v[:, None]) for v in inward(sine_y)]
    gather = [np.kron(sine_x[size_x - 2 + l][None, :], eye_y) for l in range(2)]
    gather += [np.kron(eye_x, sine_y[size_y - 2 + l][None, :]) for l in range(2)]
    edge_x = np.zeros(size_x)
    edge_x[[0, -1]] = 1.0 / 12.0
    edge_y = np.zeros(size_y)
    edge_y[[0, -1]] = 1.0 / 12.0
    edges = np.repeat((edge_x[:, None] + edge_y[None, :]).reshape(-1, 1), cells_z, axis=1)
    return (
        horizontal,
        outward,
        inverse,
        vertical,
        vertical,
        stacked(np.concatenate(spread, axis=1)[order]),
        stacked(np.concatenate(gather, axis=0)[:, order]),
        inverse_real[order],
        inverse_imag[order],
        edges[folded].astype(np.float32),
    )


def split(values):
    high = values.astype(BF16)
    return high, (values - high.astype(F32)).astype(BF16)


def product(table, values):
    high, low = split(values)
    return jnp.dot(
        table, jnp.concatenate([high, high, low], axis=0), preferred_element_type=F32
    )


def by_part(table, values):
    half = values.shape[1] // 2
    return jnp.concatenate(
        [product(table, values[:, p * half : (p + 1) * half]) for p in range(2)], axis=1
    )


def along_z(values, vertical):
    half = values.shape[1] // 2
    outs = []
    for part in range(2):
        high, low = split(values[:, part * half : (part + 1) * half])
        both = jnp.concatenate([high, low], axis=1)
        mixed = jnp.dot(both, vertical[part][...], preferred_element_type=F32)
        outs.append(mixed[:, :half] + mixed[:, half:])
    return jnp.concatenate(outs, axis=1)


def to_physical(values, tables, size_x):
    rows = values.shape[0] // 4
    step = rows * 2 // size_x
    even, odd, even_odd, odd_odd = [
        product(tables[p], values[p * rows : (p + 1) * rows]) for p in range(4)
    ]
    near, far = even + odd, even - odd
    near_odd, far_odd = even_odd + odd_odd, even_odd - odd_odd
    first = (near + near_odd, far + far_odd)
    last = (near - near_odd, far - far_odd)
    slices = [slice(i * step, (i + 1) * step) for i in range(size_x // 2)]
    pieces = [part[at] for at in slices for part in first]
    pieces += [part[at] for at in slices[::-1] for part in last]
    return jnp.concatenate(pieces, axis=0)


def to_modes(values, tables, size_x):
    step = values.shape[0] // (2 * size_x)

    def quadrant(first, half):
        ids = range(size_x // 2) if first else range(size_x - 1, size_x // 2 - 1, -1)
        starts = [(2 * i + half) * step for i in ids]
        return jnp.concatenate([values[at : at + step] for at in starts], axis=0)

    top = (quadrant(True, 0), quadrant(True, 1))
    bottom = (quadrant(False, 0), quadrant(False, 1))
    even = [t + b for t, b in zip(top, bottom)]
    odd = [t - b for t, b in zip(top, bottom)]
    folded = [even[0] + even[1], even[0] - even[1], odd[0] + odd[1], odd[0] - odd[1]]
    return jnp.concatenate([product(tables[p], folded[p]) for p in range(4)], axis=0)


def times(real, imag, values):
    half = values.shape[1] // 2
    first, second = values[:, :half], values[:, half:]
    return jnp.concatenate(
        [real * first - imag * second, real * second + imag * first], axis=1
    )


def kernel(
    grid_rows, grid_cols, cells, group,
    rs_ref, slow_ref, cells_ref, amp_ref,
    hor_ref, outw_ref, inv_ref, ver_ref, ver2_ref, spread_ref, gather_ref, lam_r, lam_i, edge_ref,
    wave_ref, resid_ref,
    fhat, spec, inner, contrast, free_out, inbound, back_x, back_y, after_x, after_y,
    medium_in, free_in, x_line, y_line, y_out, bound_hat, bound_spec,
    medium_send, medium_recv, free_send, free_recv, home_send, home_recv,
    x_send, x_recv, y_send, y_recv, back_send, back_recv,
):
    size_x, size_y, size_z = cells
    rows = size_x * size_y
    count = rs_ref.shape[0]
    row = lax.axis_index("gx")
    col = lax.axis_index("gy")
    place = row % group
    first_row = row - place
    odd = col % 2
    solves = jnp.logical_and(odd == 0, place < 4)
    own_rhs = place // 2
    own_col = col + row % 2

    def device(gx, gy):
        return {"gx": gx, "gy": gy}

    def same(gx, gy):
        return jnp.logical_and(gx == row, gy == col)

    def other(gx, gy):
        return jnp.logical_not(same(gx, gy))

    def solver(s):
        return first_row + 2 * s + odd, col - odd

    def home(k):
        return first_row + k, own_col

    has_prev = (row > 0, col > 0)
    has_next = (row < grid_rows - 1, col < grid_cols - 1)
    nexts = ((row + 1, col), (row, col + 1))
    prevs = ((row - 1, col), (row, col - 1))
    turn = row % 2
    line_prev = (row - group, col), (row + 1 - 2 * turn, col - 2 + 2 * turn)
    line_next = (row + group, col), (row + 1 - 2 * turn, col + 2 * turn)
    line_has_prev = (first_row > 0, own_col > 0)
    line_has_next = (first_row + group < grid_rows, own_col < grid_cols - 1)

    barrier = pltpu.get_barrier_semaphore()

    def greet(flag, target):
        @pl.when(flag)
        def _():
            pl.semaphore_signal(
                barrier, inc=1, device_id=device(*target), device_id_type=MESH
            )

    def number(flag):
        return flag.astype(jnp.int32)

    for s in range(count):
        greet(other(*solver(s)), solver(s))
    for axis in range(2):
        greet(has_next[axis], nexts[axis])

    @pl.when(solves)
    def _():
        for k in range(group):
            greet(other(*home(k)), home(k))
        for axis in range(2):
            greet(line_has_prev[axis], line_prev[axis])

    def copy(source, target, sent, received, peer):
        return pltpu.make_async_remote_copy(
            src_ref=source,
            dst_ref=target,
            send_sem=sent,
            recv_sem=received,
            device_id=device(*peer),
            device_id_type=MESH,
        )

    def give_medium(s):
        return copy(
            contrast, medium_in.at[place], medium_send.at[s], medium_recv.at[place], solver(s)
        )

    def give_free(s):
        return copy(
            free_out.at[s], free_in.at[place], free_send.at[s], free_recv.at[place], solver(s)
        )

    def take_medium(k):
        return copy(
            contrast, medium_in.at[k], medium_send.at[0], medium_recv.at[k], home(k)
        )

    def take_free(k):
        return copy(free_out.at[0], free_in.at[k], free_send.at[0], free_recv.at[k], home(k))

    def give_home(k, axis):
        line = (x_line, y_line)[axis]
        return copy(
            line.at[k],
            inbound.at[own_rhs, axis],
            home_send.at[k, axis],
            home_recv.at[own_rhs, axis],
            home(k),
        )

    def take_home(s, axis):
        line = (x_line, y_line)[axis]
        return copy(
            line.at[0], inbound.at[s, axis], home_send.at[0, axis], home_recv.at[s, axis],
            solver(s),
        )

    pass_x = copy(x_line.at[group], x_line.at[0], x_send, x_recv, line_next[0])

    def pass_y(k):
        return copy(y_out.at[k], y_line.at[k], y_send.at[k], y_recv.at[k], line_next[1])

    def backward(s, axis):
        source, target = ((back_x, after_x), (back_y, after_y))[axis]
        return copy(
            source.at[s], target.at[s], back_send.at[s, axis], back_recv.at[s, axis], prevs[axis]
        )

    vertical = (ver_ref, ver2_ref)

    def physical_of(values):
        return to_physical(along_z(values, vertical), outw_ref, size_x)

    def modes_of(values):
        return to_modes(along_z(values, vertical), inv_ref, size_x)

    def modes(values):
        return times(lam_r[...], lam_i[...], values)

    def load(ref):
        return jnp.concatenate([ref[0], ref[1]], axis=1)

    def save(ref, values):
        ref[0] = values[:, :size_z]
        ref[1] = values[:, size_z:]

    def through(medium, values):
        scaled = medium[...]
        return times(scaled - edge_ref[...], DAMPING * scaled, values)

    def sweeps(hat, work, medium, keep=None):
        save(work, modes(load(hat)))
        for sweep in range(2):
            physical = through(medium, physical_of(load(work)))
            if keep is not None:
                save(keep, physical)
            save(work, modes(load(hat) + modes_of(physical)))

    def traces_of(work):
        return by_part(gather_ref[...], load(work))

    def spread_of(first, second):
        return by_part(spread_ref[...], jnp.concatenate([first, second], axis=0))

    half = 2 * size_y
    upper = size_y // 2
    for t in range(upper):
        contrast[pl.ds(t, size_x, stride=size_y), :] = KAPPA * (
            slow_ref[pl.ds(t, size_x, stride=size_y), :] - 1.0
        )
        contrast[pl.ds(upper + t, size_x, stride=size_y), :] = KAPPA * (
            slow_ref[pl.ds(size_y - 1 - t, size_x, stride=size_y), :] - 1.0
        )

    row_ids = lax.broadcasted_iota(jnp.int32, (rows, size_z), 0)
    lane_ids = lax.broadcasted_iota(jnp.int32, (rows, size_z), 1)
    cell_x = row_ids // size_y + row * size_x
    cell_y = row_ids % size_y + col * size_y
    flat = (cell_x * (size_y * grid_cols) + cell_y) * size_z + lane_ids

    def forcing(s):
        real = rs_ref[s, 0]
        imag = rs_ref[s, 1]
        for p in range(cells_ref.shape[1]):
            hit = flat == cells_ref[s, p]
            real = real + jnp.where(hit, amp_ref[s, 0, p], 0.0)
            imag = imag + jnp.where(hit, amp_ref[s, 1, p], 0.0)
        return jnp.concatenate([real, imag], axis=1)

    peers = sum(number(other(*solver(s))) for s in range(count))
    peers = peers + sum(number(flag) for flag in has_prev)
    line_peers = sum(number(other(*home(k))) for k in range(group))
    line_peers = line_peers + sum(number(flag) for flag in line_has_next)
    pl.semaphore_wait(barrier, peers + jnp.where(solves, line_peers, 0))

    def if_other(flag_target, action):
        @pl.when(other(*flag_target))
        def _():
            action()

    for s in range(count):
        if_other(solver(s), give_medium(s).start)

    @pl.when(solves)
    def _():
        @pl.when(first_row == 0)
        def _():
            x_line[0] = jnp.zeros_like(x_line[0])

        @pl.when(own_col == 0)
        def _():
            y_line[...] = jnp.zeros_like(y_line)

    def prepare(step, _):
        s = count - 1 - step
        hat = product(hor_ref[...], along_z(forcing(s), vertical))
        save(fhat.at[s], hat)
        sweeps(fhat.at[s], spec.at[s], contrast)
        out = traces_of(spec.at[s])
        free_out[s, 0] = out[:half]
        free_out[s, 1] = out[half:]
        if_other(solver(s), give_free(s).start)
        return 0

    lax.fori_loop(0, count, prepare, 0)

    def advance(k, _):
        tile_row, tile_col = home(k)
        mine = same(tile_row, tile_col)

        @pl.when(mine)
        def _():
            medium_in[k] = contrast[...]
            free_in[k] = free_out[own_rhs]

        @pl.when(own_col > 0)
        def _():
            pass_y(k).wait_recv()

        @pl.when(jnp.logical_and(k == 0, first_row > 0))
        def _():
            pass_x.wait_recv()

        @pl.when(mine)
        def _():
            inbound[own_rhs, 0] = x_line[k]
            inbound[own_rhs, 1] = y_line[k]

        @pl.when(jnp.logical_not(mine))
        def _():
            for axis in range(2):
                give_home(k, axis).start()
            take_medium(k).wait_recv()
            take_free(k).wait_recv()

        start = jnp.logical_and(tile_row == 0, tile_col == 0)
        end = jnp.logical_and(tile_row == grid_rows - 1, tile_col == grid_cols - 1)

        @pl.when(start)
        def _():
            x_line[k + 1] = free_in[k, 0]
            y_out[k] = free_in[k, 1]

        @pl.when(jnp.logical_not(jnp.logical_or(start, end)))
        def _():
            save(bound_hat, spread_of(x_line[k], y_line[k]))
            sweeps(bound_hat, bound_spec, medium_in.at[k])
            out = traces_of(bound_spec)
            x_line[k + 1] = free_in[k, 0] + out[:half]
            y_out[k] = free_in[k, 1] + out[half:]

        @pl.when(line_has_next[1])
        def _():
            pass_y(k).start()

        @pl.when(jnp.logical_and(k == group - 1, line_has_next[0]))
        def _():
            pass_x.start()
        return 0

    @pl.when(solves)
    def _():
        lax.fori_loop(0, group, advance, 0)

    def unfold(target, source, s, c):
        for t in range(upper):
            low = pl.ds(t, size_x, stride=size_y)
            target[s, c, low, :] = source[s, c, low, :]
            high = pl.ds(size_y - 1 - t, size_x, stride=size_y)
            target[s, c, high, :] = source[s, c, pl.ds(upper + t, size_x, stride=size_y), :]

    def finish(step, _):
        s = count - 1 - step

        @pl.when(other(*solver(s)))
        def _():
            for axis in range(2):
                take_home(s, axis).wait_recv()

        save(fhat.at[s], load(fhat.at[s]) + spread_of(inbound[s, 0], inbound[s, 1]))
        sweeps(fhat.at[s], spec.at[s], contrast, inner.at[s])
        wave = physical_of(load(spec.at[s]))
        save(inner.at[s], through(contrast, wave) - load(inner.at[s]))
        save(spec.at[s], wave)
        for c in range(2):
            lanes = slice(c * size_z, (c + 1) * size_z)
            unfold(wave_ref, spec, s, c)
            back_x[s, :, lanes] = wave_ref[s, c, :half]
            for l in range(2):
                back_y[s, l, :, lanes] = wave_ref[s, c, pl.ds(l, size_x, stride=size_y), :]
        for axis in range(2):
            @pl.when(has_prev[axis])
            def _():
                backward(s, axis).start()
        return 0

    lax.fori_loop(0, count, finish, 0)

    def close(step, _):
        s = count - 1 - step
        for c in range(2):
            unfold(resid_ref, inner, s, c)

        @pl.when(has_next[0])
        def _():
            backward(s, 0).wait_recv()
            near = after_x[s, :size_y]
            far = after_x[s, size_y:]
            for c in range(2):
                lanes = slice(c * size_z, (c + 1) * size_z)
                resid_ref[s, c, rows - 2 * size_y : rows - size_y] -= near[:, lanes] / 12.0
                resid_ref[s, c, rows - size_y :] += (16.0 * near - far)[:, lanes] / 12.0

        @pl.when(has_next[1])
        def _():
            backward(s, 1).wait_recv()
            near = after_y[s, 0]
            far = after_y[s, 1]
            for c in range(2):
                lanes = slice(c * size_z, (c + 1) * size_z)
                below = pl.ds(size_y - 2, size_x, stride=size_y)
                last = pl.ds(size_y - 1, size_x, stride=size_y)
                resid_ref[s, c, below, :] = resid_ref[s, c, below, :] - near[:, lanes] / 12.0
                resid_ref[s, c, last, :] = (
                    resid_ref[s, c, last, :] + (16.0 * near - far)[:, lanes] / 12.0
                )

        @pl.when(other(*solver(s)))
        def _():
            give_medium(s).wait_send()
            give_free(s).wait_send()

        for axis in range(2):
            @pl.when(has_prev[axis])
            def _():
                backward(s, axis).wait_send()
        return 0

    lax.fori_loop(0, count, close, 0)

    @pl.when(solves)
    def _():
        @pl.when(line_has_next[0])
        def _():
            pass_x.wait_send()

        def settle(k, _):
            @pl.when(other(*home(k)))
            def _():
                for axis in range(2):
                    give_home(k, axis).wait_send()

            @pl.when(line_has_next[1])
            def _():
                pass_y(k).wait_send()
            return 0

        lax.fori_loop(0, group, settle, 0)


def solution(mesh):
    grid_rows, grid_cols = mesh.shape["gx"], mesh.shape["gy"]
    group = 4

    def body(right_side, slowness, source_cells, source_amplitudes):
        count, parts, size_x, size_y, size_z = right_side.shape
        rows = size_x * size_y
        wide = 2 * size_z
        tables = build_tables(size_x, size_y, size_z)
        dma = pltpu.SemaphoreType.DMA

        def field(*lead):
            return pltpu.VMEM((*lead, 2, rows, size_z), F32)

        def traces(*lead):
            return pltpu.VMEM((*lead, 2 * size_y, wide), F32)

        full = pl.BlockSpec(memory_space=pltpu.VMEM)
        scalars = pl.BlockSpec(memory_space=pltpu.SMEM)
        block = jax.ShapeDtypeStruct((count, parts, rows, size_z), F32)
        wave, resid = pl.pallas_call(
            functools.partial(kernel, grid_rows, grid_cols, (size_x, size_y, size_z), group),
            out_shape=(block, block),
            in_specs=[full, full, scalars, scalars] + [full] * len(tables),
            out_specs=(full, full),
            scratch_shapes=[
                field(count),
                field(count),
                field(count),
                pltpu.VMEM((rows, size_z), F32),
                traces(count, 2),
                traces(count, 2),
                traces(count),
                pltpu.VMEM((count, 2, size_x, wide), F32),
                traces(count),
                pltpu.VMEM((count, 2, size_x, wide), F32),
                pltpu.VMEM((group, rows, size_z), F32),
                traces(group, 2),
                traces(group + 1),
                traces(group),
                traces(group),
                field(),
                field(),
                dma((count,)),
                dma((group,)),
                dma((count,)),
                dma((group,)),
                dma((group, 2)),
                dma((count, 2)),
                dma,
                dma,
                dma((group,)),
                dma((group,)),
                dma((count, 2)),
                dma((count, 2)),
            ],
            compiler_params=pltpu.CompilerParams(collective_id=0, has_side_effects=True),
        )(
            right_side.reshape(count, parts, rows, size_z),
            slowness.reshape(rows, size_z),
            source_cells,
            source_amplitudes.transpose(0, 2, 1),
            *[jnp.asarray(t) for t in tables],
        )
        shape = (count, parts, size_x, size_y, size_z)
        return (wave.reshape(shape), resid.reshape(shape))

    return jax.shard_map(
        body,
        mesh=mesh,
        in_specs=(P(None, None, "gx", "gy", None), P("gx", "gy", None), P(), P()),
        out_specs=(P(None, None, "gx", "gy", None), P(None, None, "gx", "gy", None)),
        check_vma=False,
    )
```

time: 121 us -> 86.2 us (0.71)
  Pallas kernels: 116 us -> 82.7 us
  local copies, waits for them, and re-layouts: 4.14 us -> 2.72 us
    pallas_call x1, Pallas kernels: 116 us -> 82.7 us  [body(): pl.pallas_call(functools.partial(kernel, grid_rows, grid_cols, (size_x, s...]
    unnamed x7 -> x4, local copies, waits for them, and re-layouts: 3.49 us -> 2.72 us
where the time goes in v2:
time: 86.2 us; the launch traced here: 86 us
  Pallas kernels  82.7 us (96%)
  local copies, waits for them, and re-layouts  2.72 us (3%)
    pallas_call x1, Pallas kernels, body(): pl.pallas_call(functools.partial(kernel, grid_rows, grid_cols, (size_x, s...  82.7 us
    unnamed x4, local copies, waits for them, and re-layouts  2.72 us

profile of v2, /device:TPU:119, one launch (start us, length us, event | category | flops | bytes accessed | tf_op | source)
XLA Modules:
  0.0 86.0 jit_solution(3015068699781929465)
XLA Ops:
  0.6 82.7 %shard_map.140 = (f32[2,2,256,128]{3,2,1,0:T(8,128)}, f32[2,2,256,128]{3,2,1,0:T(8,128)}) custom-call(f32[2,2,256,128]{3,2,1,0:T(8,128)} %bitcast.5, f32[256,128]{1,0:T(8,128)} %bitcast.8, s32[2,16]{1,0:T(2,128)} %cells_ref.1, f32[2,2,16]{2,1,0:T(2,128)} %bitcast.9, bf16[256,768]{1,0:T(8,128)(2,1)} %constant.18.clone.hor_ref, ...), custom_call_target="tpu_custom_call" | custom-call | tf_op jit(solution)/shard_map/pallas_call | solution.py:559
  83.3 0.0 copy-start
  83.3 1.9 %copy.17 = f32[2,2,16,16,128]{4,3,2,1,0:T(8,128)} copy(f32[2,2,16,16,128]{4,3,2,1,0:T(8,128)} %bitcast.7) | data formatting | bytes 1048576
  85.2 0.0 copy-done
  85.2 0.8 copy.18
Async XLA Ops:
  83.3 1.9 %copy-start = (f32[2,2,256,128]{3,2,1,0:T(8,128)S(1)}, f32[2,2,256,128]{3,2,1,0:T(8,128)}, u32[]{:S(2)}) copy-start(f32[2,2,256,128]{3,2,1,0:T(8,128)} %get-tuple-element.5) | copy-start | bytes 1572868

commit v3 on v2

--- a/solution.py
+++ b/solution.py
@@ -55,7 +55,6 @@
     ]
     outward = np.stack([stacked(block) for block in blocks])
     inverse = np.stack([stacked(block.T) for block in blocks])
-    horizontal = stacked(np.kron(sine_x, sine_y)[order])
     high, low = split_table(sine_z)
     vertical = np.concatenate([np.concatenate([high, low], axis=1)] * 2, axis=0)
     eye_x = np.eye(size_x)
@@ -74,7 +73,6 @@
     edge_y[[0, -1]] = 1.0 / 12.0
     edges = np.repeat((edge_x[:, None] + edge_y[None, :]).reshape(-1, 1), cells_z, axis=1)
     return (
-        horizontal,
         outward,
         inverse,
         vertical,
@@ -158,12 +156,12 @@
 
 
 def kernel(
-    grid_rows, grid_cols, cells, group,
+    load_inputs, put_wave, put_resid, grid_rows, grid_cols, cells, group,
     rs_ref, slow_ref, cells_ref, amp_ref,
-    hor_ref, outw_ref, inv_ref, ver_ref, ver2_ref, spread_ref, gather_ref, lam_r, lam_i, edge_ref,
+    outw_ref, inv_ref, ver_ref, ver2_ref, spread_ref, gather_ref, lam_r, lam_i, edge_ref,
     wave_ref, resid_ref,
-    fhat, spec, inner, contrast, free_out, inbound, back_x, back_y, after_x, after_y,
-    medium_in, free_in, x_line, y_line, y_out, bound_hat, bound_spec,
+    fhat, spec, inner, contrast, medium, free_out, inbound, back_x, back_y, after_x, after_y,
+    medium_in, free_in, x_line, y_line, y_out, bound_hat, bound_spec, line_medium,
     medium_send, medium_recv, free_send, free_recv, home_send, home_recv,
     x_send, x_recv, y_send, y_recv, back_send, back_recv,
 ):
@@ -175,9 +173,10 @@
     place = row % group
     first_row = row - place
     odd = col % 2
-    solves = jnp.logical_and(odd == 0, place < 4)
+    pair = col // 2
+    solves = jnp.logical_and(odd != pair % 2, place < 4)
     own_rhs = place // 2
-    own_col = col + row % 2
+    own_col = 2 * pair + row % 2
 
     def device(gx, gy):
         return {"gx": gx, "gy": gy}
@@ -188,19 +187,24 @@
     def other(gx, gy):
         return jnp.logical_not(same(gx, gy))
 
-    def solver(s):
-        return first_row + 2 * s + odd, col - odd
+    def solver(s, tile_col=col):
+        group_col = tile_col - tile_col % 2
+        return first_row + 2 * s + tile_col % 2, group_col + 1 - group_col // 2 % 2
 
     def home(k):
         return first_row + k, own_col
+
+    def side(k):
+        return first_row + k, own_col + 1
 
     has_prev = (row > 0, col > 0)
     has_next = (row < grid_rows - 1, col < grid_cols - 1)
     nexts = ((row + 1, col), (row, col + 1))
     prevs = ((row - 1, col), (row, col - 1))
     turn = row % 2
-    line_prev = (row - group, col), (row + 1 - 2 * turn, col - 2 + 2 * turn)
-    line_next = (row + group, col), (row + 1 - 2 * turn, col + 2 * turn)
+    near = pair % 2
+    line_prev = (row - group, col), (row + 1 - 2 * turn, col - (1 - turn) * (3 - 2 * near))
+    line_next = (row + group, col), (row + 1 - 2 * turn, col + turn * (1 + 2 * near))
     line_has_prev = (first_row > 0, own_col > 0)
     line_has_next = (first_row + group < grid_rows, own_col < grid_cols - 1)
 
@@ -216,8 +220,10 @@
     def number(flag):
         return flag.astype(jnp.int32)
 
+    before = jnp.maximum(col - 1, 0)
     for s in range(count):
         greet(other(*solver(s)), solver(s))
+        greet(jnp.logical_and(col > 0, other(*solver(s, before))), solver(s, before))
     for axis in range(2):
         greet(has_next[axis], nexts[axis])
 
@@ -227,6 +233,8 @@
             greet(other(*home(k)), home(k))
         for axis in range(2):
             greet(line_has_prev[axis], line_prev[axis])
+
+    load_inputs()
 
     def copy(source, target, sent, received, peer):
         return pltpu.make_async_remote_copy(
@@ -256,18 +264,26 @@
     def take_free(k):
         return copy(free_out.at[0], free_in.at[k], free_send.at[0], free_recv.at[k], home(k))
 
-    def give_home(k, axis):
-        line = (x_line, y_line)[axis]
+    def give_home(k):
         return copy(
-            line.at[k],
-            inbound.at[own_rhs, axis],
-            home_send.at[k, axis],
-            home_recv.at[own_rhs, axis],
+            x_line.at[k],
+            inbound.at[own_rhs, 0],
+            home_send.at[k, 0],
+            home_recv.at[own_rhs, 0],
             home(k),
         )
 
+    def pass_side(k):
+        return copy(
+            y_out.at[k],
+            inbound.at[own_rhs, 1],
+            home_send.at[k, 1],
+            home_recv.at[own_rhs, 1],
+            side(k),
+        )
+
     def take_home(s, axis):
-        line = (x_line, y_line)[axis]
+        line = (x_line, y_out)[axis]
         return copy(
             line.at[0], inbound.at[s, axis], home_send.at[0, axis], home_recv.at[s, axis],
             solver(s),
@@ -302,14 +318,17 @@
         ref[0] = values[:, :size_z]
         ref[1] = values[:, size_z:]
 
-    def through(medium, values):
-        scaled = medium[...]
-        return times(scaled - edge_ref[...], DAMPING * scaled, values)
-
-    def sweeps(hat, work, medium, keep=None):
+    def through(factor, values):
+        return times(factor[0], factor[1], values)
+
+    def factors(target, scaled):
+        target[0] = scaled - edge_ref[...]
+        target[1] = DAMPING * scaled
+
+    def sweeps(hat, work, factor, keep=None):
         save(work, modes(load(hat)))
         for sweep in range(2):
-            physical = through(medium, physical_of(load(work)))
+            physical = through(factor, physical_of(load(work)))
             if keep is not None:
                 save(keep, physical)
             save(work, modes(load(hat) + modes_of(physical)))
@@ -329,35 +348,66 @@
         contrast[pl.ds(upper + t, size_x, stride=size_y), :] = KAPPA * (
             slow_ref[pl.ds(size_y - 1 - t, size_x, stride=size_y), :] - 1.0
         )
-
-    row_ids = lax.broadcasted_iota(jnp.int32, (rows, size_z), 0)
-    lane_ids = lax.broadcasted_iota(jnp.int32, (rows, size_z), 1)
-    cell_x = row_ids // size_y + row * size_x
-    cell_y = row_ids % size_y + col * size_y
-    flat = (cell_x * (size_y * grid_cols) + cell_y) * size_z + lane_ids
+    factors(medium, contrast[...])
+
+    points = cells_ref.shape[1]
+    row_ids = lax.broadcasted_iota(jnp.int32, (rows, points), 0)
+    in_row = row_ids % size_y
+    in_row = jnp.where(in_row < upper, in_row, size_y + upper - 1 - in_row)
+    row_ids = row_ids - row_ids % size_y + in_row
+    lane_ids = lax.broadcasted_iota(jnp.int32, (size_z, points), 0)
+
+    def fold(s):
+        for c in range(2):
+            for t in range(upper):
+                low = pl.ds(t, size_x, stride=size_y)
+                inner[s, c, low, :] = rs_ref[s, c, low, :]
+                high = pl.ds(size_y - 1 - t, size_x, stride=size_y)
+                inner[s, c, pl.ds(upper + t, size_x, stride=size_y), :] = rs_ref[s, c, high, :]
 
     def forcing(s):
-        real = rs_ref[s, 0]
-        imag = rs_ref[s, 1]
-        for p in range(cells_ref.shape[1]):
-            hit = flat == cells_ref[s, p]
-            real = real + jnp.where(hit, amp_ref[s, 0, p], 0.0)
-            imag = imag + jnp.where(hit, amp_ref[s, 1, p], 0.0)
-        return jnp.concatenate([real, imag], axis=1)
+        fold(s)
+        flat = cells_ref[pl.ds(s, 1), :]
+        at_x = flat // (size_y * grid_cols * size_z) - row * size_x
+        at_y = flat // size_z % (size_y * grid_cols) - col * size_y
+        inside = jnp.logical_and(
+            jnp.logical_and(at_x >= 0, at_x < size_x), jnp.logical_and(at_y >= 0, at_y < size_y)
+        )
+        at_row = jnp.where(inside, at_x * size_y + at_y, -1)
+        where_row = jnp.where(row_ids == at_row, 1.0, 0.0).astype(BF16)
+        hit_z = lane_ids == flat % size_z
+        outs = []
+        for c in range(2):
+            rest = jnp.where(hit_z, amp_ref[s, c : c + 1, :], 0.0)
+            total = inner[s, c]
+            for term in range(3):
+                part = rest.astype(BF16)
+                rest = rest - part.astype(F32)
+                total = total + lax.dot_general(
+                    where_row, part, (((1,), (1,)), ((), ())), preferred_element_type=F32
+                )
+            outs.append(total)
+        return jnp.concatenate(outs, axis=1)
 
     peers = sum(number(other(*solver(s))) for s in range(count))
     peers = peers + sum(number(flag) for flag in has_prev)
     line_peers = sum(number(other(*home(k))) for k in range(group))
     line_peers = line_peers + sum(number(flag) for flag in line_has_next)
-    pl.semaphore_wait(barrier, peers + jnp.where(solves, line_peers, 0))
+    line_peers = line_peers + sum(
+        number(jnp.logical_and(line_has_next[1], other(*side(k)))) for k in range(group)
+    )
 
     def if_other(flag_target, action):
         @pl.when(other(*flag_target))
         def _():
             action()
 
-    for s in range(count):
-        if_other(solver(s), give_medium(s).start)
+    early = jnp.logical_and(col < grid_cols // 2, jnp.logical_or(place < 2, col == 0))
+    corner = jnp.logical_and(row == 0, col == 0)
+
+    @pl.when(col == 0)
+    def _():
+        inbound[:, 1] = jnp.zeros_like(inbound[:, 1])
 
     @pl.when(solves)
     def _():
@@ -369,71 +419,112 @@
         def _():
             y_line[...] = jnp.zeros_like(y_line)
 
+    def rank(step):
+        return jnp.where(place < 2, count - 1 - step, step)
+
+    def open_sends():
+        pl.semaphore_wait(barrier, peers + jnp.where(solves, line_peers, 0))
+        for s in range(count):
+            @pl.when(jnp.logical_and(early, jnp.logical_and(other(*solver(s)), ~corner)))
+            def _():
+                give_medium(s).start()
+
+        if_other(solver(rank(0)), give_free(rank(0)).start)
+
     def prepare(step, _):
-        s = count - 1 - step
-        hat = product(hor_ref[...], along_z(forcing(s), vertical))
-        save(fhat.at[s], hat)
-        sweeps(fhat.at[s], spec.at[s], contrast)
+        s = rank(step)
+
+        @pl.when(step == 1)
+        def _():
+            open_sends()
+
+        save(fhat.at[s], modes_of(forcing(s)))
+        sweeps(fhat.at[s], spec.at[s], medium)
         out = traces_of(spec.at[s])
         free_out[s, 0] = out[:half]
         free_out[s, 1] = out[half:]
-        if_other(solver(s), give_free(s).start)
+
+        @pl.when(jnp.logical_and(step == 1, other(*solver(s))))
+        def _():
+            give_free(s).start()
         return 0
 
     lax.fori_loop(0, count, prepare, 0)
+    for s in range(count):
+        @pl.when(jnp.logical_and(~early, other(*solver(s))))
+        def _():
+            give_medium(s).start()
 
     def advance(k, _):
         tile_row, tile_col = home(k)
         mine = same(tile_row, tile_col)
 
-        @pl.when(mine)
-        def _():
-            medium_in[k] = contrast[...]
-            free_in[k] = free_out[own_rhs]
-
-        @pl.when(own_col > 0)
-        def _():
-            pass_y(k).wait_recv()
-
-        @pl.when(jnp.logical_and(k == 0, first_row > 0))
-        def _():
-            pass_x.wait_recv()
-
-        @pl.when(mine)
-        def _():
-            inbound[own_rhs, 0] = x_line[k]
-            inbound[own_rhs, 1] = y_line[k]
-
-        @pl.when(jnp.logical_not(mine))
-        def _():
-            for axis in range(2):
-                give_home(k, axis).start()
-            take_medium(k).wait_recv()
-            take_free(k).wait_recv()
-
         start = jnp.logical_and(tile_row == 0, tile_col == 0)
         end = jnp.logical_and(tile_row == grid_rows - 1, tile_col == grid_cols - 1)
 
+        @pl.when(mine)
+        def _():
+            free_in[k] = free_out[own_rhs]
+            line_medium[...] = medium[...]
+
+        @pl.when(jnp.logical_not(jnp.logical_or(mine, start)))
+        def _():
+            take_medium(k).wait_recv()
+            factors(line_medium, medium_in[k])
+
+        @pl.when(jnp.logical_and(k == 0, first_row > 0))
+        def _():
+            pass_x.wait_recv()
+
+        @pl.when(mine)
+        def _():
+            inbound[own_rhs, 0] = x_line[k]
+
+        @pl.when(jnp.logical_not(mine))
+        def _():
+            give_home(k).start()
+
+        @pl.when(own_col > 0)
+        def _():
+            pass_y(k).wait_recv()
+
+        @pl.when(jnp.logical_not(jnp.logical_or(start, end)))
+        def _():
+            save(bound_hat, spread_of(x_line[k], y_line[k]))
+            sweeps(bound_hat, bound_spec, line_medium)
+            out = traces_of(bound_spec)
+            x_line[k + 1] = out[:half]
+            y_out[k] = out[half:]
+
         @pl.when(start)
         def _():
-            x_line[k + 1] = free_in[k, 0]
-            y_out[k] = free_in[k, 1]
-
-        @pl.when(jnp.logical_not(jnp.logical_or(start, end)))
-        def _():
-            save(bound_hat, spread_of(x_line[k], y_line[k]))
-            sweeps(bound_hat, bound_spec, medium_in.at[k])
-            out = traces_of(bound_spec)
-            x_line[k + 1] = free_in[k, 0] + out[:half]
-            y_out[k] = free_in[k, 1] + out[half:]
+            x_line[k + 1] = jnp.zeros_like(x_line[k])
+            y_out[k] = jnp.zeros_like(y_out[k])
+
+        @pl.when(jnp.logical_not(mine))
+        def _():
+            take_free(k).wait_recv()
+
+        @pl.when(jnp.logical_not(end))
+        def _():
+            x_line[k + 1] += free_in[k, 0]
+            y_out[k] += free_in[k, 1]
+
+        @pl.when(jnp.logical_and(k == group - 1, line_has_next[0]))
+        def _():
+            pass_x.start()
 
         @pl.when(line_has_next[1])
         def _():
             pass_y(k).start()
 
-        @pl.when(jnp.logical_and(k == group - 1, line_has_next[0]))
-        def _():
-            pass_x.start()
+            @pl.when(other(*side(k)))
+            def _():
+                pass_side(k).start()
+
+            @pl.when(same(*side(k)))
+            def _():
+                inbound[own_rhs, 1] = y_out[k]
         return 0
 
     @pl.when(solves)
@@ -452,13 +543,16 @@
 
         @pl.when(other(*solver(s)))
         def _():
-            for axis in range(2):
-                take_home(s, axis).wait_recv()
+            take_home(s, 0).wait_recv()
+
+        @pl.when(jnp.logical_and(col > 0, other(*solver(s, before))))
+        def _():
+            take_home(s, 1).wait_recv()
 
         save(fhat.at[s], load(fhat.at[s]) + spread_of(inbound[s, 0], inbound[s, 1]))
-        sweeps(fhat.at[s], spec.at[s], contrast, inner.at[s])
+        sweeps(fhat.at[s], spec.at[s], medium, inner.at[s])
         wave = physical_of(load(spec.at[s]))
-        save(inner.at[s], through(contrast, wave) - load(inner.at[s]))
+        save(inner.at[s], through(medium, wave) - load(inner.at[s]))
         save(spec.at[s], wave)
         for c in range(2):
             lanes = slice(c * size_z, (c + 1) * size_z)
@@ -466,6 +560,7 @@
             back_x[s, :, lanes] = wave_ref[s, c, :half]
             for l in range(2):
                 back_y[s, l, :, lanes] = wave_ref[s, c, pl.ds(l, size_x, stride=size_y), :]
+        put_wave(s).start()
         for axis in range(2):
             @pl.when(has_prev[axis])
             def _():
@@ -503,10 +598,15 @@
                     resid_ref[s, c, last, :] + (16.0 * near - far)[:, lanes] / 12.0
                 )
 
+        put_resid(s).start()
+
         @pl.when(other(*solver(s)))
         def _():
+            give_free(s).wait_send()
+
+        @pl.when(jnp.logical_and(other(*solver(s)), ~corner))
+        def _():
             give_medium(s).wait_send()
-            give_free(s).wait_send()
 
         for axis in range(2):
             @pl.when(has_prev[axis])
@@ -516,6 +616,13 @@
 
     lax.fori_loop(0, count, close, 0)
 
+    def flush(s, _):
+        put_wave(s).wait()
+        put_resid(s).wait()
+        return 0
+
+    lax.fori_loop(0, count, flush, 0)
+
     @pl.when(solves)
     def _():
         @pl.when(line_has_next[0])
@@ -525,15 +632,43 @@
         def settle(k, _):
             @pl.when(other(*home(k)))
             def _():
-                for axis in range(2):
-                    give_home(k, axis).wait_send()
+                give_home(k).wait_send()
 
             @pl.when(line_has_next[1])
             def _():
                 pass_y(k).wait_send()
+
+                @pl.when(other(*side(k)))
+                def _():
+                    pass_side(k).wait_send()
             return 0
 
         lax.fori_loop(0, group, settle, 0)
+
+
+def staged(sizes, inputs, *refs):
+    sources, refs = refs[:inputs], refs[inputs:]
+    wave_out, resid_out, refs = refs[0], refs[1], refs[2:]
+    targets, refs = refs[:inputs], refs[inputs:]
+    wave, resid, in_sem, wave_sem, resid_sem, refs = *refs[:5], refs[5:]
+
+    def load_inputs():
+        copies = [
+            pltpu.make_async_copy(source, target, in_sem.at[i])
+            for i, (source, target) in enumerate(zip(sources, targets))
+        ]
+        for copy in copies:
+            copy.start()
+        for copy in copies:
+            copy.wait()
+
+    def put_wave(s):
+        return pltpu.make_async_copy(wave.at[s], wave_out.at[s], wave_sem.at[s])
+
+    def put_resid(s):
+        return pltpu.make_async_copy(resid.at[s], resid_out.at[s], resid_sem.at[s])
+
+    kernel(load_inputs, put_wave, put_resid, *sizes, *targets, wave, resid, *refs)
 
 
 def solution(mesh):
@@ -553,19 +688,30 @@
         def traces(*lead):
             return pltpu.VMEM((*lead, 2 * size_y, wide), F32)
 
-        full = pl.BlockSpec(memory_space=pltpu.VMEM)
-        scalars = pl.BlockSpec(memory_space=pltpu.SMEM)
+        whole = pl.BlockSpec(memory_space=pl.ANY)
         block = jax.ShapeDtypeStruct((count, parts, rows, size_z), F32)
+        operands = (
+            right_side.reshape(count, parts, rows, size_z),
+            slowness.reshape(rows, size_z),
+            source_cells,
+            source_amplitudes.transpose(0, 2, 1),
+            *[jnp.asarray(t) for t in tables],
+        )
+        sizes = (grid_rows, grid_cols, (size_x, size_y, size_z), group)
         wave, resid = pl.pallas_call(
-            functools.partial(kernel, grid_rows, grid_cols, (size_x, size_y, size_z), group),
+            functools.partial(staged, sizes, len(operands)),
             out_shape=(block, block),
-            in_specs=[full, full, scalars, scalars] + [full] * len(tables),
-            out_specs=(full, full),
-            scratch_shapes=[
+            in_specs=[whole] * len(operands),
+            out_specs=(whole, whole),
+            scratch_shapes=[pltpu.VMEM(o.shape, o.dtype) for o in operands]
+            + [pltpu.VMEM(block.shape, F32)] * 2
+            + [dma((len(operands),)), dma((count,)), dma((count,))]
+            + [
                 field(count),
                 field(count),
                 field(count),
                 pltpu.VMEM((rows, size_z), F32),
+                field(),
                 traces(count, 2),
                 traces(count, 2),
                 traces(count),
@@ -577,6 +723,7 @@
                 traces(group + 1),
                 traces(group),
                 traces(group),
+                field(),
                 field(),
                 field(),
                 dma((count,)),
@@ -593,13 +740,7 @@
                 dma((count, 2)),
             ],
             compiler_params=pltpu.CompilerParams(collective_id=0, has_side_effects=True),
-        )(
-            right_side.reshape(count, parts, rows, size_z),
-            slowness.reshape(rows, size_z),
-            source_cells,
-            source_amplitudes.transpose(0, 2, 1),
-            *[jnp.asarray(t) for t in tables],
-        )
+        )(*operands)
         shape = (count, parts, size_x, size_y, size_z)
         return (wave.reshape(shape), resid.reshape(shape))
 

time: 86.2 us -> 84.5 us (0.980)
  Pallas kernels: 82.7 us -> 80.7 us
    pallas_call x1, Pallas kernels: 82.7 us -> 80.7 us  [body(): pl.pallas_call(functools.partial(staged, sizes, len(operands)), out_shape...]
where the time goes in v3:
time: 84.5 us; the launch traced here: 84 us
  Pallas kernels  80.7 us (96%)
  local copies, waits for them, and re-layouts  2.72 us (3%)
    pallas_call x1, Pallas kernels, body(): pl.pallas_call(functools.partial(staged, sizes, len(operands)), out_shape...  80.7 us
    unnamed x4, local copies, waits for them, and re-layouts  2.72 us

profile of v3, /device:TPU:119, one launch (start us, length us, event | category | flops | bytes accessed | tf_op | source)
XLA Modules:
  0.0 84.0 jit_solution(10244354159096897582)
XLA Ops:
  0.6 80.7 %shard_map.131 = (f32[2,2,256,128]{3,2,1,0:T(8,128)}, f32[2,2,256,128]{3,2,1,0:T(8,128)}) custom-call(f32[2,2,256,128]{3,2,1,0:T(8,128)} %bitcast.7, f32[256,128]{1,0:T(8,128)} %bitcast.8, s32[2,16]{1,0:T(2,128)} %refs_2_.1, f32[2,2,16]{2,1,0:T(2,128)} %bitcast.9, bf16[4,64,192]{2,1,0:T(8,128)(2,1)} %constant.16.clone.refs_4_, ...), custom_call_target="tpu_custom_call" | custom-call | tf_op jit(solution)/shard_map/pallas_call | solution.py:701
  81.3 0.0 copy-start
  81.3 1.9 %copy.16 = f32[2,2,16,16,128]{4,3,2,1,0:T(8,128)} copy(f32[2,2,16,16,128]{4,3,2,1,0:T(8,128)} %bitcast.6) | data formatting | bytes 1048576
  83.2 0.0 copy-done
  83.2 0.8 copy.17
Async XLA Ops:
  81.3 1.9 %copy-start = (f32[2,2,256,128]{3,2,1,0:T(8,128)S(1)}, f32[2,2,256,128]{3,2,1,0:T(8,128)}, u32[]{:S(2)}) copy-start(f32[2,2,256,128]{3,2,1,0:T(8,128)} %get-tuple-element.5) | copy-start | bytes 1572868

commit v4 on v3

--- a/solution.py
+++ b/solution.py
@@ -156,7 +156,7 @@
 
 
 def kernel(
-    load_inputs, put_wave, put_resid, grid_rows, grid_cols, cells, group,
+    load_inputs, grid_rows, grid_cols, cells, group,
     rs_ref, slow_ref, cells_ref, amp_ref,
     outw_ref, inv_ref, ver_ref, ver2_ref, spread_ref, gather_ref, lam_r, lam_i, edge_ref,
     wave_ref, resid_ref,
@@ -560,7 +560,6 @@
             back_x[s, :, lanes] = wave_ref[s, c, :half]
             for l in range(2):
                 back_y[s, l, :, lanes] = wave_ref[s, c, pl.ds(l, size_x, stride=size_y), :]
-        put_wave(s).start()
         for axis in range(2):
             @pl.when(has_prev[axis])
             def _():
@@ -598,8 +597,6 @@
                     resid_ref[s, c, last, :] + (16.0 * near - far)[:, lanes] / 12.0
                 )
 
-        put_resid(s).start()
-
         @pl.when(other(*solver(s)))
         def _():
             give_free(s).wait_send()
@@ -616,12 +613,6 @@
 
     lax.fori_loop(0, count, close, 0)
 
-    def flush(s, _):
-        put_wave(s).wait()
-        put_resid(s).wait()
-        return 0
-
-    lax.fori_loop(0, count, flush, 0)
 
     @pl.when(solves)
     def _():
@@ -648,9 +639,9 @@
 
 def staged(sizes, inputs, *refs):
     sources, refs = refs[:inputs], refs[inputs:]
-    wave_out, resid_out, refs = refs[0], refs[1], refs[2:]
+    wave, resid, refs = refs[0], refs[1], refs[2:]
     targets, refs = refs[:inputs], refs[inputs:]
-    wave, resid, in_sem, wave_sem, resid_sem, refs = *refs[:5], refs[5:]
+    in_sem, refs = refs[0], refs[1:]
 
     def load_inputs():
         copies = [
@@ -662,18 +653,12 @@
         for copy in copies:
             copy.wait()
 
-    def put_wave(s):
-        return pltpu.make_async_copy(wave.at[s], wave_out.at[s], wave_sem.at[s])
-
-    def put_resid(s):
-        return pltpu.make_async_copy(resid.at[s], resid_out.at[s], resid_sem.at[s])
-
-    kernel(load_inputs, put_wave, put_resid, *sizes, *targets, wave, resid, *refs)
+    kernel(load_inputs, *sizes, *targets, wave, resid, *refs)
 
 
 def solution(mesh):
     grid_rows, grid_cols = mesh.shape["gx"], mesh.shape["gy"]
-    group = 4
+    group = 8
 
     def body(right_side, slowness, source_cells, source_amplitudes):
         count, parts, size_x, size_y, size_z = right_side.shape
@@ -700,12 +685,11 @@
         sizes = (grid_rows, grid_cols, (size_x, size_y, size_z), group)
         wave, resid = pl.pallas_call(
             functools.partial(staged, sizes, len(operands)),
-            out_shape=(block, block),
+            out_shape=(pltpu.VMEM(block.shape, F32), pltpu.VMEM(block.shape, F32)),
             in_specs=[whole] * len(operands),
-            out_specs=(whole, whole),
+            out_specs=(pl.BlockSpec(memory_space=pltpu.VMEM),) * 2,
             scratch_shapes=[pltpu.VMEM(o.shape, o.dtype) for o in operands]
-            + [pltpu.VMEM(block.shape, F32)] * 2
-            + [dma((len(operands),)), dma((count,)), dma((count,))]
+            + [dma((len(operands),))]
             + [
                 field(count),
                 field(count),

time: 84.5 us -> 79.6 us (0.942)
  Pallas kernels: 80.7 us -> 76.5 us
  local copies, waits for them, and re-layouts: 2.72 us -> 1.59 us
    pallas_call x1, Pallas kernels: 80.7 us -> 76.5 us  [body(): pl.pallas_call(functools.partial(staged, sizes, len(operands)), out_shape...]
    unnamed x4 -> x2, local copies, waits for them, and re-layouts: 2.72 us -> 1.59 us
where the time goes in v4:
time: 79.6 us; the launch traced here: 78.7 us
  Pallas kernels  76.5 us (96%)
  local copies, waits for them, and re-layouts  1.59 us (2%)
    pallas_call x1, Pallas kernels, body(): pl.pallas_call(functools.partial(staged, sizes, len(operands)), out_shape...  76.5 us

profile of v4, /device:TPU:119, one launch (start us, length us, event | category | flops | bytes accessed | tf_op | source)
XLA Modules:
  0.0 78.7 jit_solution(18231685670171638149)
XLA Ops:
  0.6 76.5 %shard_map.131 = (f32[2,2,256,128]{3,2,1,0:T(8,128)S(1)}, f32[2,2,256,128]{3,2,1,0:T(8,128)S(1)}) custom-call(f32[2,2,256,128]{3,2,1,0:T(8,128)} %bitcast.7, f32[256,128]{1,0:T(8,128)} %bitcast.8, s32[2,16]{1,0:T(2,128)} %refs_2_.1, f32[2,2,16]{2,1,0:T(2,128)} %bitcast.9, bf16[4,64,192]{2,1,0:T(8,128)(2,1)} %constant.16.clone.refs_4_, ...), custom_call_target="tpu_custom_call" | custom-call | tf_op jit(solution)/shard_map/pallas_call | solution.py:686
  77.1 0.8 %copy.16 = f32[2,2,16,16,128]{4,3,2,1,0:T(8,128)} copy(f32[2,2,16,16,128]{4,3,2,1,0:T(8,128)S(1)} %bitcast.6) | data formatting | bytes 1048576
  77.9 0.8 %copy.17 = f32[2,2,16,16,128]{4,3,2,1,0:T(8,128)} copy(f32[2,2,16,16,128]{4,3,2,1,0:T(8,128)S(1)} %bitcast.5) | data formatting | bytes 1048576
